TPU v7x, 128 devices: a whole 4x4x4 slice. The times are simulated.
128 devices in a mesh: row: 8 (over z, y_lo), col: 16 (over y_hi, x, core).
Axes of the slice: x: 4, y: 4 (y_hi: 2, y_lo: 2; y = y_hi * 2 + y_lo), z: 4, core: 2. Of those that a mesh axis runs over, the one named last changes fastest.
Arguments:
- stiffness: float32 [4, 8, 512, 2, 16, 512], P(None, 'row', None, None, 'col'), may hold values from -7 to 7
- lower_panel: float32 [4, 8, 512, 512], P(None, 'row'), may hold values from -0.25 to 0.25
- diag_inverse: float32 [512, 512], replicated, as said below
Outputs:
- reduced: float32 [4, 8, 512, 2, 16, 512], P(None, 'row', None, None, 'col')
Inputs may be any that keep to these rules, and one draw needn't show every extreme that they name: diag_inverse is lower triangular with a positive diagonal.
All inputs are finite; a program needn't handle non-finite values.
Results may differ from a plain program's by a relative error of at most 0.000062.
Values sent between devices are 32-bit elements; how exact they have to be, the bound alone decides.
A program may use at most 128 MiB of HBM per device.

v0:
```python
import jax
import jax.numpy as jnp
from jax import lax
from jax.sharding import PartitionSpec as P


def spread(value, axis, source):
    kept = jnp.where(lax.axis_index(axis) == source, value, 0).astype(value.dtype)
    return lax.psum(kept, axis)


def body(stiffness, lower_panel, diag_inverse):
    highest = lax.Precision.HIGHEST
    rows = lax.axis_size("row")
    cols = lax.axis_size("col")
    my_row = lax.axis_index("row")
    my_col = lax.axis_index("col")
    blocks = stiffness[:, 0, :, :, 0, :]
    brows = blocks.shape[0]
    width = blocks.shape[1]
    bcols = blocks.shape[2]
    row_ids = jnp.arange(brows) * rows + my_row
    keep_rows = (row_ids != 0)[:, None, None]
    lower_rows = jnp.where(keep_rows, lower_panel[:, 0], 0.0)
    column_zero = spread(blocks[:, :, 0, :], "col", 0)
    corner_source = column_zero[0]
    corner = spread(corner_source, "row", 0)
    c_block = jnp.dot(
        jnp.dot(diag_inverse, corner, precision=highest), diag_inverse.T, precision=highest
    )
    panel_rows = jnp.where(keep_rows, column_zero, 0.0)
    lower_c_rows = jnp.einsum("bik,kj->bij", lower_rows, c_block, precision=highest)
    w_rows = (
        jnp.einsum("bik,jk->bij", panel_rows, diag_inverse, precision=highest) - 0.5 * lower_c_rows
    )
    final_rows = w_rows - 0.5 * lower_c_rows
    ratio = cols // rows
    source = my_col % rows
    offset = my_col // rows
    values = jnp.concatenate([w_rows, lower_rows], axis=2)
    grouped = values.reshape(bcols, ratio, width, values.shape[-1])
    joined = spread(lax.dynamic_index_in_dim(grouped, offset, 1, keepdims=False), "row", source)
    w_cols = joined[:, :, :width]
    lower_cols = joined[:, :, width:]
    lower_c_cols = jnp.einsum("bik,kj->bij", lower_cols, c_block, precision=highest)
    update = blocks - jnp.einsum("bik,cjk->bicj", w_rows, lower_cols, precision=highest)
    update = update - jnp.einsum("bik,cjk->bicj", lower_rows, w_cols, precision=highest)
    final_cols = w_cols - 0.5 * lower_c_cols
    first_column = jnp.where(my_col == 0, final_rows, update[:, :, 0, :])
    update = update.at[:, :, 0, :].set(first_column)
    first_row = jnp.where(my_row == 0, jnp.transpose(final_cols, (2, 0, 1)), update[0])
    update = update.at[0].set(first_row)
    at_corner = jnp.logical_and(my_row == 0, my_col == 0)
    update = update.at[0, :, 0, :].set(jnp.where(at_corner, c_block, update[0, :, 0, :]))
    return update[:, None, :, :, None, :]


def solution(mesh):
    in_specs = (P(None, "row", None, None, "col", None), P(None, "row", None, None), P())
    out_specs = P(None, "row", None, None, "col", None)
    return jax.shard_map(body, mesh=mesh, in_specs=in_specs, out_specs=out_specs, check_vma=False)
```

profile of v0, /device:TPU:1, one launch (start us, length us, event | category | flops | bytes accessed | tf_op | source)
XLA Modules:
  0.0 576.5 jit_solution(12848044044958805449)
XLA Ops:
  6.5 0.0 copy-start
  6.5 0.0 all-reduce.4.cloned.1.call-start
  6.5 20.6 %copy.17 = f32[4,1,512,2,1,512]{2,5,0,3,4,1:T(8,128)} copy(f32[4,1,512,2,1,512]{5,4,3,2,1,0:T(1,128)} %param.9) | data formatting | bytes 16777216 | tf_op args[0]
  27.1 4.7 fusion.3
  31.8 0.0 all-reduce.4.cloned.1.call-update
  31.8 0.0 all-reduce.6.cloned.1.call-start
  31.9 153.0 %all-reduce.4.cloned.1.call-done = f32[4,512,512]{1,2,0:T(8,128)} async-done(((f32[4,512,512]{1,2,0:T(8,128)}), f32[4,512,512]{1,2,0:T(8,128)}) %all-reduce.4.cloned.1.call-update) | async-done | bytes 4194320 | tf_op jit(solution)/shard_map/psum | solution.py:9
  184.9 2.3 fusion.28
  187.2 0.0 all-reduce.6.cloned.1.call-update
  187.2 0.0 all-reduce.8.cloned.1.call-start
  187.3 5.3 copy.19
  192.6 4.8 bitcast_select_fusion
  197.3 68.0 %all-reduce.6.cloned.1.call-done = f32[512,512]{0,1:T(8,128)} async-done(((f32[512,512]{0,1:T(8,128)}), f32[512,512]{0,1:T(8,128)}) %all-reduce.6.cloned.1.call-update) | async-done | bytes 1048592 | tf_op jit(solution)/shard_map/psum | solution.py:9
  265.4 0.0 copy-done
  265.4 0.0 copy-start.2
  265.4 3.2 fusion.34
  268.6 3.5 fusion.35
  272.1 0.0 copy-done.2
  272.1 0.0 copy-start.8
  272.1 8.2 %fusion.30 = f32[4,512,512]{1,2,0:T(8,128)S(1)} fusion(f32[4,512,512]{1,2,0:T(8,128)S(1)} %copy-done.2, f32[512,512]{1,0:T(8,128)S(1)} %fusion.35), kind=kOutput, calls=%fused_computation.35 | convolution fusion | flops 6442450944 | bytes 9437184 | tf_op jit(solution)/shard_map/bik,kj->bij/dot_general | solution.py:32
  280.4 0.0 copy-start.5
  280.4 2.0 copy-done.5
  282.3 0.0 copy-done.8
  282.3 8.6 %multiply_subtract_fusion = f32[4,512,512]{1,2,0:T(8,128)S(1)} fusion(f32[4,512,512]{1,2,0:T(8,128)S(1)} %fusion.30, f32[4,512,512]{1,2,0:T(8,128)S(1)} %copy-done.8, pred[4]{0:T(512)(128)(4,1)S(1)} %add_compare_fusion, f32[512,512]{1,0:T(8,128)S(1)} %copy-done), kind=kOutput, calls=%fused_computation.16 | convolution fusion | flops 6445596672 | bytes 13631492 | tf_op jit(solution)/shard_map/bik,jk->bij/dot_general | solution.py:34
  291.0 0.0 copy-start.3
  291.0 4.5 pad_maximum_fusion
  295.4 0.0 copy-done.3
  295.4 4.6 constant_dynamic-slice_fusion
  300.0 5.6 copy.46
  305.6 2.8 select_bitcast_fusion
  308.4 0.0 all-reduce.8.cloned.1.call-update
  308.4 0.3 copy.29
  308.8 187.6 %all-reduce.8.cloned.1.call-done = f32[2,512,1024]{2,1,0:T(8,128)} async-done(((f32[2,512,1024]{2,1,0:T(8,128)}), f32[2,512,1024]{2,1,0:T(8,128)}) %all-reduce.8.cloned.1.call-update) | async-done | bytes 4194320 | tf_op jit(solution)/shard_map/psum | solution.py:9
  496.3 0.0 copy-start.4
  496.3 18.6 %fusion.4 = f32[4,512,2,512]{1,3,0,2:T(8,128)} fusion(f32[4,512,512]{1,2,0:T(8,128)} %bitcast_select_fusion, f32[2,512,1024]{2,1,0:T(8,128)} %all-reduce.8.cloned.1.call-done), kind=kOutput, calls=%fused_computation.8 | convolution fusion | flops 12884901888 | bytes 14680064 | tf_op jit(solution)/shard_map/bik,cjk->bicj/dot_general | solution.py:47
  514.9 0.0 copy-done.4
  514.9 0.0 copy-start.6
  514.9 20.6 %subtract_subtract_fusion = f32[4,512,2,512]{1,3,0,2:T(8,128)S(1)} fusion(f32[4,512,2,512]{1,3,0,2:T(8,128)} %fusion.4, f32[4,512,512]{1,2,0:T(8,128)S(1)} %copy-done.4, f32[2,512,1024]{2,1,0:T(8,128)} %all-reduce.8.cloned.1.call-done, f32[4,1,512,2,1,512]{2,5,0,3,4,1:T(8,128)} %copy.17), kind=kOutput, calls=%fused_computation.1 | convolution fusion | flops 12889096192 | bytes 31457280 | tf_op jit(solution)/shard_map/bik,cjk->bicj/dot_general | solution.py:46
  535.5 0.0 copy-done.6
  535.5 2.2 fusion.2
  537.7 0.0 copy-start.7
  537.7 4.3 copy.51
  542.0 1.0 copy-done.7
  542.9 4.9 bitcast_dynamic-update-slice_fusion
  547.9 0.0 copy-start.1
  547.9 1.2 fusion.27
  549.1 20.5 %copy.31 = f32[4,1,512,2,1,512]{5,4,3,2,1,0:T(1,128)} copy(f32[4,1,512,2,1,512]{2,5,0,3,4,1:T(8,128)} %fusion.27) | data formatting | bytes 16777216 | tf_op jit(solution)/shard_map/scatter | solution.py:54
  569.6 0.0 copy-done.1
  (1 shorter events, 0.0 us)
Async XLA Ops:
  6.5 258.8 %copy-start = (f32[512,512]{1,0:T(8,128)S(1)}, f32[512,512]{1,0:T(8,128)}, u32[]{:S(2)}) copy-start(f32[512,512]{1,0:T(8,128)} %param.11) | copy-start | bytes 3145732
  6.5 178.3 %all-reduce.4.cloned.1.call-start = ((), (), s32[]{:S(2)}) async-start(), calls=%async_computation | async-start | bytes 8388608 | tf_op jit(solution)/shard_map/psum | solution.py:9
  31.8 233.5 %all-reduce.6.cloned.1.call-start = ((), (), s32[]{:S(2)}) async-start(), calls=%async_computation.1 | async-start | bytes 2097152 | tf_op jit(solution)/shard_map/psum | solution.py:9
  187.2 309.1 %all-reduce.8.cloned.1.call-start = ((), (), s32[]{:S(2)}) async-start(), calls=%async_computation.2 | async-start | bytes 8388608 | tf_op jit(solution)/shard_map/psum | solution.py:9
  265.4 6.7 %copy-start.2 = (f32[4,512,512]{1,2,0:T(8,128)S(1)}, f32[4,512,512]{1,2,0:T(8,128)}, u32[]{:S(2)}) copy-start(f32[4,512,512]{1,2,0:T(8,128)} %bitcast_select_fusion) | copy-start | bytes 12582916
  272.1 10.2 %copy-start.8 = (f32[4,512,512]{1,2,0:T(8,128)S(1)}, f32[4,512,512]{1,2,0:T(8,128)}, u32[]{:S(2)}) copy-start(f32[4,512,512]{1,2,0:T(8,128)} %all-reduce.4.cloned.1.call-done) | copy-start | bytes 12582916
  280.4 2.0 copy-start.5
  291.0 4.5 copy-start.3
  496.3 18.6 %copy-start.4 = (f32[4,512,512]{1,2,0:T(8,128)S(1)}, f32[4,512,512]{1,2,0:T(8,128)}, u32[]{:S(2)}) copy-start(f32[4,512,512]{1,2,0:T(8,128)} %copy-done.3) | copy-start | bytes 12582916
  514.9 20.6 %copy-start.6 = (f32[4,512,512]{1,2,0:T(8,128)S(1)}, f32[4,512,512]{1,2,0:T(8,128)}, u32[]{:S(2)}) copy-start(f32[4,512,512]{1,2,0:T(8,128)} %copy-done.5) | copy-start | bytes 12582916
  537.7 5.2 copy-start.7
  547.9 21.7 %copy-start.1 = (f32[512,512]{1,0:T(8,128)S(1)}, f32[512,512]{1,0:T(8,128)}, u32[]{:S(2)}) copy-start(f32[512,512]{1,0:T(8,128)} %param.11) | copy-start | bytes 3145732
Sparse Core Ops, SparseCore 0:
  31.9 152.8 all-reduce.3
  187.4 77.9 all-reduce.5
  308.6 187.7 all-reduce.7
where the time goes:
time: 587 us; the launch traced here: 577 us
  waiting for transfers between devices  409 us (70%)
  matrix products  67.7 us (12%)
  local copies, waits for them, and re-layouts  64.1 us (11%)
  other arithmetic  22.3 us (4%)
  between operations  13.7 us (2%)
    psum x3, waiting for transfers between devices, spread(): return lax.psum(kept, axis)  409 us
    unnamed x22, local copies, waits for them, and re-layouts  38.7 us
    dot_general x1, matrix products, body(): jnp.einsum('bik,cjk->bicj', w_rows, lower_cols, precision=highest)  20.6 us
    scatter x1, local copies, waits for them, and re-layouts, body(): update.at[0, :, 0, :].set(jnp.where(at_corner, c_block, update[0, :, 0, :]))  20.5 us
    dot_general x1, matrix products, body(): jnp.einsum('bik,cjk->bicj', lower_rows, w_cols, precision=highest)  18.6 us
  transfers between devices with their start and end apart: 3, of which 3 were waited for; matrix products, arithmetic and copies ran while one was open for 2% of the time, Pallas kernels for 0%

commit v1 on v0

v1 whole, which is shorter than its diff:
```python
import functools

import jax
import jax.numpy as jnp
from jax import lax
from jax.experimental import pallas as pl
from jax.experimental.pallas import tpu as pltpu
from jax.sharding import PartitionSpec as P

F32, BF = jnp.float32, jnp.bfloat16
MESH = pl.DeviceIdType.MESH
NT = (((1,), (1,)), ((), ()))
NN = (((1,), (0,)), ((), ()))
PIECES = 16
CHUNKS = 8


def split(x):
    high = x.astype(BF)
    return high, (x - high.astype(F32)).astype(BF)


def dot3(ah, al, bh, bl, dims):
    dot = functools.partial(
        lax.dot_general, dimension_numbers=dims, preferred_element_type=F32
    )
    return dot(ah, bh) + dot(ah, bl) + dot(al, bh)


def gather_kernel(
    a, low, dinv, qi, lj, qj, raw, turned, dh, dl, send_sems, recv_sems, local_sems
):
    row, col = lax.axis_index("row"), lax.axis_index("col")
    z, yl = row // 2, lax.rem(row, 2)
    yh, x, k = col // 8, lax.rem(col // 2, 4), lax.rem(col, 2)
    y = 2 * yh + yl
    nb = dinv.shape[0]
    part = nb // PIECES

    def at(dx=0, dy=0, dz=0, dk=0):
        nx, ny = lax.rem(x + dx + 4, 4), lax.rem(y + dy + 4, 4)
        nz, nk = lax.rem(z + dz + 4, 4), lax.rem(k + dk, 2)
        return (2 * nz + lax.rem(ny, 2), 8 * (ny // 2) + 2 * nx + nk)

    used = {"send": 0, "recv": 0, "local": 0}
    open_sends = []

    def take(kind, count=1):
        first = used[kind]
        used[kind] += count
        return first

    def when(cond, body):
        if cond is None:
            body()
        else:
            pl.when(cond)(body)

    def send(cond, src, dst, recv, device):
        sem = take("send")

        def copy():
            return pltpu.make_async_remote_copy(
                src_ref=src,
                dst_ref=dst,
                send_sem=send_sems.at[sem],
                recv_sem=recv_sems.at[recv],
                device_id=device,
                device_id_type=MESH,
            )

        when(cond, lambda: copy().start())
        open_sends.append((cond, lambda: copy().wait_send()))

    def arrive(cond, dst, recv):
        def body():
            pltpu.make_async_remote_copy(
                src_ref=dst,
                dst_ref=dst,
                send_sem=send_sems.at[0],
                recv_sem=recv_sems.at[recv],
                device_id=at(dk=1),
                device_id_type=MESH,
            ).wait_recv()

        when(cond, body)

    barrier = pltpu.get_barrier_semaphore()

    def greet(cond, device):
        when(
            cond,
            lambda: pl.semaphore_signal(
                barrier, inc=1, device_id=device, device_id_type=MESH
            ),
        )

    neighbours = [at(dx=1), at(dx=3), at(dy=1), at(dy=3), at(dz=1), at(dz=3), at(dy=2), at(dk=1)]
    for device in neighbours:
        greet(None, device)
    greet(col != 0, (row, 0))
    greet(row != 0, (0, col))
    greet(None, (0, lax.rem(col + 8, PIECES)))
    expect = (
        len(neighbours)
        + jnp.where(col == 0, PIECES - 1, 0)
        + jnp.where(row == 0, 7 + 8, 0)
    )
    pl.semaphore_wait(barrier, expect)

    raw_recv = take("recv")
    for piece in range(1, PIECES):
        send(
            col == 0,
            a.at[:, pl.ds(piece * part, part), 0],
            raw,
            raw_recv,
            (row, piece),
        )
    own_raw = pltpu.make_async_copy(
        a.at[:, pl.ds(0, part), 0], raw, local_sems.at[take("local")]
    )
    pl.when(col == 0)(lambda: own_raw.start())

    dz = lax.rem(z - x + 4, 4)
    size = nb // CHUNKS

    def exchange(source, target):
        root = dz == 0
        mine = jnp.logical_and(root, yl == k)
        other = jnp.logical_and(root, yl != k)
        cross = take("recv", 2 * CHUNKS)
        ring = take("recv", 2 * CHUNKS)
        keep = [
            pltpu.make_async_copy(
                source.at[2 * c + yh], target.at[c], local_sems.at[take("local")]
            )
            for c in range(2)
        ]

        def rows(s):
            return pl.ds(s * size, size)

        def start():
            @pl.when(mine)
            def _():
                for copy in keep:
                    copy.start()

            for s in range(CHUNKS):
                for c, dy in ((0, 1), (1, 3)):
                    their = lax.rem(y + dy, 4) // 2
                    send(
                        mine,
                        source.at[2 * c + their, rows(s)],
                        target.at[c, rows(s)],
                        cross + c * CHUNKS + s,
                        at(dy=dy),
                    )
                    send(
                        mine,
                        source.at[2 * c + yh, rows(s)],
                        target.at[c, rows(s)],
                        ring + c * CHUNKS + s,
                        at(dz=1 if c == 0 else 3),
                    )

        def step(s):
            for c in range(2):
                here = target.at[c, rows(s)]
                arrive(other, here, cross + c * CHUNKS + s)
                arrive(dz != 0, here, ring + c * CHUNKS + s)
                last = dz == (3 if c == 0 else 1)
                send(
                    jnp.logical_and(jnp.logical_not(mine), jnp.logical_not(last)),
                    here,
                    here,
                    ring + c * CHUNKS + s,
                    at(dz=1 if c == 0 else 3),
                )

        def finish():
            @pl.when(mine)
            def _():
                for copy in keep:
                    copy.wait()

        return start, step, finish

    l_start, l_step, l_finish = exchange(low, lj)
    l_start()

    dh[...], dl[...] = split(dinv[...])
    arrive(col != 0, raw, raw_recv)
    pl.when(col == 0)(lambda: own_raw.wait())

    for b in range(4):
        rows = jnp.concatenate([raw[b, :, t, :] for t in range(4)], axis=1)
        high, lo = split(rows)
        turned[b] = dot3(high, lo, dh[...], dl[...], NT)
    turned[4] = turned[0]

    def slab(piece, count=5):
        return qi.at[pl.ds(0, count), pl.ds(pl.multiple_of(piece * part, part), part)]

    head = take("recv")
    head2 = take("recv")
    pair = take("recv")
    partner = lax.rem(col + 8, PIECES)
    send(None, turned.at[pl.ds(0, 4)], slab(col, 4), pair, at(dy=2))
    my_head = qi.at[4, pl.ds(pl.multiple_of(col * part, part), part)]
    for r in range(8):
        if r:
            send(row == 0, turned.at[4], my_head, head, (r, col))
        send(row == 0, turned.at[4], my_head, head2, (r, partner))
    keep4 = pltpu.make_async_copy(
        turned.at[pl.ds(0, 4)], slab(col, 4), local_sems.at[take("local")]
    )
    keep4.start()
    keep1 = pltpu.make_async_copy(turned.at[4], my_head, local_sems.at[take("local")])
    pl.when(row == 0)(lambda: keep1.start())

    for s in range(CHUNKS // 2):
        l_step(s)

    arrive(None, slab(partner, 4), pair)
    arrive(row != 0, my_head, head)
    arrive(None, qi.at[4, pl.ds(pl.multiple_of(partner * part, part), part)], head2)
    keep4.wait()
    pl.when(row == 0)(lambda: keep1.wait())

    def near(piece, dx):
        return 8 * (piece // 8) + 2 * lax.rem(x + dx, 4) + k

    right = take("recv", 2)
    left = take("recv", 2)
    far = take("recv", 2)
    core = take("recv", 8)
    both = (8 * 0 + 2 * x + k, 8 + 2 * x + k)
    for h in range(2):
        send(None, slab(both[h]), slab(both[h]), right + h, at(dx=1))
        send(None, slab(both[h]), slab(both[h]), left + h, at(dx=3))
    for h in range(2):
        send(None, slab(both[h]), slab(both[h]), core + h, at(dk=1))
    for s in range(CHUNKS // 2, CHUNKS):
        l_step(s)
    for h in (0, 1):
        from_left, from_right = near(both[h], 3), near(both[h], 1)
        arrive(None, slab(from_left), right + h)
        if h == 0:
            send(None, slab(from_left), slab(from_left), far, at(dx=1))
        send(None, slab(from_left), slab(from_left), core + 2 + h, at(dk=1))
        arrive(None, slab(from_right), left + h)
        if h == 1:
            send(None, slab(from_right), slab(from_right), far + 1, at(dx=3))
        send(None, slab(from_right), slab(from_right), core + 4 + h, at(dk=1))
    for h in (0, 1):
        opposite = near(both[h], 2)
        arrive(None, slab(opposite), far + h)
        send(None, slab(opposite), slab(opposite), core + 6 + h, at(dk=1))
    for n, dx in enumerate((0, 3, 1, 2)):
        for h in range(2):
            theirs = 8 * h + 2 * lax.rem(x + dx, 4) + lax.rem(k + 1, 2)
            arrive(None, slab(theirs), core + 2 * n + h)

    l_finish()
    q_start, q_step, q_finish = exchange(qi, qj)
    q_start()
    for s in range(CHUNKS):
        q_step(s)
    q_finish()
    for cond, body in open_sends:
        when(cond, body)
    assert used["send"] <= send_sems.shape[0], used
    assert used["recv"] <= recv_sems.shape[0], used
    assert used["local"] <= local_sems.shape[0], used


def gather(a, low, dinv):
    nb = dinv.shape[0]
    part = nb // PIECES
    anywhere = pl.BlockSpec(memory_space=pltpu.HBM)
    return pl.pallas_call(
        gather_kernel,
        out_shape=(
            jax.ShapeDtypeStruct((5, nb, nb), F32),
            jax.ShapeDtypeStruct((2, nb, nb), F32),
            jax.ShapeDtypeStruct((2, nb, nb), F32),
        ),
        in_specs=[anywhere, anywhere, pl.BlockSpec(memory_space=pltpu.VMEM)],
        out_specs=(anywhere, anywhere, anywhere),
        scratch_shapes=[
            pltpu.VMEM((4, part, 4, 128), F32),
            pltpu.VMEM((5, part, nb), F32),
            pltpu.VMEM((nb, nb), BF),
            pltpu.VMEM((nb, nb), BF),
            pltpu.SemaphoreType.DMA((160,)),
            pltpu.SemaphoreType.DMA((90,)),
            pltpu.SemaphoreType.DMA((10,)),
        ],
        compiler_params=pltpu.CompilerParams(
            collective_id=0, has_side_effects=True, vmem_limit_bytes=16 << 20
        ),
        name="gather",
    )(a, low, dinv)


def update_kernel(a, qi, li, lj, qj, r, dinv, o, yh, yl, ch, cl, sh, sl, cf, xh, xl):
    b = pl.program_id(0)
    row, col = lax.axis_index("row"), lax.axis_index("col")

    @pl.when(b == 0)
    def _():
        @pl.loop(0, 2)
        def _(c):
            rows = pl.ds(pl.multiple_of(c * 512, 512), 512)
            yh[rows, :512], yl[rows, :512] = split(lj[c])
            yh[rows, 512:], yl[rows, 512:] = split(qj[c])

        dh, dl = split(dinv[...])
        rh, rl = split(r[0])
        cf[...] = dot3(dh, dl, rh, rl, NN)
        ch[...], cl[...] = split(cf[...])
        sh[...], sl[...] = split(0.5 * (cf[...] + cf[...].T))

    xh[:, 512:], xl[:, 512:] = split(li[0])

    @pl.loop(0, 2)
    def _(m):
        rows = pl.ds(pl.multiple_of(m * 256, 256), 256)
        f = qi[0, rows, :] - dot3(xh[rows, 512:], xl[rows, 512:], sh[...], sl[...], NN)
        xh[rows, :512], xl[rows, :512] = split(f)

    @pl.loop(0, 4)
    def _(n):
        c, half = n // 2, lax.rem(n, 2)
        rows = pl.ds(pl.multiple_of(n * 256, 256), 256)
        cols = pl.ds(pl.multiple_of(half * 256, 256), 256)
        top = jnp.logical_and(row == 0, b == 0)
        side = jnp.logical_and(col == 0, c == 0)

        def put(values):
            for t in range(2):
                o[pl.ds(n * 2 + t, 512, stride=8), :] = values(t)

        @pl.when(jnp.logical_not(jnp.logical_or(top, side)))
        def _():
            acc = dot3(xh[...], xl[...], yh[rows, :], yl[rows, :], NT)
            put(
                lambda t: a[pl.ds(n * 2 + t, 512, stride=8), :]
                - acc[:, t * 128 : (t + 1) * 128]
            )

        @pl.when(jnp.logical_and(side, jnp.logical_not(top)))
        def _():
            fin = qi[0, :, cols] - dot3(
                xh[:, 512:], xl[:, 512:], ch[:, cols], cl[:, cols], NN
            )
            put(lambda t: fin[:, t * 128 : (t + 1) * 128])

        @pl.when(jnp.logical_and(top, jnp.logical_not(side)))
        def _():
            fin = qj[c, cols, :] - dot3(
                yh[rows, :512], yl[rows, :512], ch[...], cl[...], NN
            )
            fin = fin.T
            put(lambda t: fin[:, t * 128 : (t + 1) * 128])

        @pl.when(jnp.logical_and(top, side))
        def _():
            fin = cf[:, cols]
            put(lambda t: fin[:, t * 128 : (t + 1) * 128])


def update(a, qi, li, lj, qj, dinv):
    nb = dinv.shape[0]
    pairs = pl.BlockSpec((2, nb, nb), lambda b: (0, 0, 0))
    block = pl.BlockSpec((1, nb, nb), lambda b: (b, 0, 0))
    linear = pl.BlockSpec((8 * nb, 128), lambda b: (b, 0))
    return pl.pallas_call(
        update_kernel,
        grid=(4,),
        out_shape=jax.ShapeDtypeStruct(a.shape, F32),
        in_specs=[
            linear,
            block,
            block,
            pairs,
            pairs,
            pl.BlockSpec((1, nb, nb), lambda b: (4, 0, 0)),
            pl.BlockSpec((nb, nb), lambda b: (0, 0)),
        ],
        out_specs=linear,
        scratch_shapes=[pltpu.VMEM((2 * nb, 2 * nb), BF)] * 2
        + [pltpu.VMEM((nb, nb), BF)] * 4
        + [pltpu.VMEM((nb, nb), F32)]
        + [pltpu.VMEM((nb, 2 * nb), BF)] * 2,
        compiler_params=pltpu.CompilerParams(vmem_limit_bytes=56 << 20),
        name="update",
    )(a, qi, li, lj, qj, qi, dinv)


def body(stiffness, lower_panel, diag_inverse):
    shape = stiffness.shape
    tiles = stiffness.reshape(4, 512, 2, 4, 128)
    rows = stiffness.reshape(16384, 128)
    low = lower_panel[:, 0]
    qi, lj, qj = gather(tiles, low, diag_inverse)
    out = update(rows, qi, low, lj, qj, diag_inverse)
    return out.reshape(shape)


def solution(mesh):
    in_specs = (P(None, "row", None, None, "col", None), P(None, "row", None, None), P())
    out_specs = P(None, "row", None, None, "col", None)
    return jax.shard_map(body, mesh=mesh, in_specs=in_specs, out_specs=out_specs, check_vma=False)
```

time: 587 us -> 363 us (0.62)
  the two profiles are of different devices: /device:TPU:1 before, /device:TPU:28 now
where the time goes in v1:
time: 363 us
  Pallas kernels  351 us (97%)
  local copies, waits for them, and re-layouts  11.8 us (3%)
    pallas_call x1, Pallas kernels, gather(): pl.pallas_call(gather_kernel, out_shape=(jax.ShapeDtypeStruct((5, nb, nb)...  321 us
    pallas_call x1, Pallas kernels, update(): pl.pallas_call(update_kernel, grid=(4,), out_shape=jax.ShapeDtypeStruct(a...  30 us
    unnamed x12, local copies, waits for them, and re-layouts  11.8 us

profile of v1, /device:TPU:28, one launch (start us, length us, event | category | flops | bytes accessed | tf_op | source)
XLA Modules:
  0.0 363.0 jit_solution(16050276508863373210)
XLA Ops:
  0.0 0.0 copy-start
  0.0 3.4 copy-done
  3.4 0.0 copy-start.2
  3.4 2.2 copy-done.2
  5.6 0.0 copy-start.3
  5.6 1.2 copy-done.3
  6.8 321.2 %gather.1 = (f32[5,512,512]{2,1,0:T(8,128)S(1)}, f32[2,512,512]{2,1,0:T(8,128)S(1)}, f32[2,512,512]{2,1,0:T(8,128)S(1)}) custom-call(f32[4,512,2,4,128]{4,3,2,1,0:T(4,128)S(1)} %bitcast.5, f32[4,512,512]{2,1,0:T(8,128)S(1)} %bitcast.7, f32[512,512]{1,0:T(8,128)S(1)} %copy-done.3), custom_call_target="tpu_custom_call" | custom-call | tf_op jit(solution)/shard_map/gather/pallas_call | solution.py:283
  328.0 0.0 copy-start.1
  328.0 2.3 copy-done.1
  330.3 0.0 copy-start.4
  330.3 1.4 copy-done.4
  331.6 0.0 copy-start.5
  331.6 1.4 copy-done.5
  333.0 30.0 %update.1 = f32[16384,128]{1,0:T(8,128)} custom-call(f32[16384,128]{1,0:T(8,128)} %bitcast.4, f32[5,512,512]{2,1,0:T(8,128)} %copy-done.1, f32[4,512,512]{2,1,0:T(8,128)} %bitcast.6, f32[2,512,512]{2,1,0:T(8,128)} %copy-done.4, f32[2,512,512]{2,1,0:T(8,128)} %copy-done.5, f32[5,512,512]{2,1,0:T(8,128)} %copy-done.1, f32[512,512]{1,0:T(8,128)} %dinv.3), custom_call_target="tpu_custom_call" | custom-call | tf_op jit(solution)/shard_map/update/pallas_call | solution.py:380
Async XLA Ops:
  0.0 3.4 copy-start
  3.4 2.2 copy-start.2
  5.6 1.2 copy-start.3
  328.0 2.3 copy-start.1
  330.3 1.4 copy-start.4
  331.6 1.4 copy-start.5

commit v2 on v1

--- a/solution.py
+++ b/solution.py
@@ -28,7 +28,7 @@
 
 
 def gather_kernel(
-    a, low, dinv, qi, lj, qj, raw, turned, dh, dl, send_sems, recv_sems, local_sems
+    a, low, dinv, qi_out, lj_out, qj_out, raw, turned, dh, dl, qi, lj, qj, send_sems, recv_sems, local_sems
 ):
     row, col = lax.axis_index("row"), lax.axis_index("col")
     z, yl = row // 2, lax.rem(row, 2)
@@ -56,7 +56,7 @@
         else:
             pl.when(cond)(body)
 
-    def send(cond, src, dst, recv, device):
+    def send(tag, cond, src, dst, recv, device):
         sem = take("send")
 
         def copy():
@@ -72,7 +72,7 @@
         when(cond, lambda: copy().start())
         open_sends.append((cond, lambda: copy().wait_send()))
 
-    def arrive(cond, dst, recv):
+    def arrive(tag, cond, dst, recv):
         def body():
             pltpu.make_async_remote_copy(
                 src_ref=dst,
@@ -84,6 +84,9 @@
             ).wait_recv()
 
         when(cond, body)
+
+    def keep(src, dst):
+        return pltpu.make_async_copy(src, dst, local_sems.at[take("local")])
 
     barrier = pltpu.get_barrier_semaphore()
 
@@ -111,46 +114,42 @@
     raw_recv = take("recv")
     for piece in range(1, PIECES):
         send(
+            "S",
             col == 0,
             a.at[:, pl.ds(piece * part, part), 0],
             raw,
             raw_recv,
             (row, piece),
         )
-    own_raw = pltpu.make_async_copy(
-        a.at[:, pl.ds(0, part), 0], raw, local_sems.at[take("local")]
-    )
+    own_raw = keep(a.at[:, pl.ds(0, part), 0], raw)
     pl.when(col == 0)(lambda: own_raw.start())
 
     dz = lax.rem(z - x + 4, 4)
     size = nb // CHUNKS
 
-    def exchange(source, target):
-        root = dz == 0
-        mine = jnp.logical_and(root, yl == k)
-        other = jnp.logical_and(root, yl != k)
+    def exchange(tag, source, target):
+        mine = jnp.logical_and(dz == 0, yl == k)
         cross = take("recv", 2 * CHUNKS)
         ring = take("recv", 2 * CHUNKS)
-        keep = [
-            pltpu.make_async_copy(
-                source.at[2 * c + yh], target.at[c], local_sems.at[take("local")]
-            )
-            for c in range(2)
-        ]
+        own = [keep(source.at[2 * c + yh], target.at[c]) for c in range(2)]
+        hops = (dz, lax.rem(4 - dz, 4))
+        up = (at(dz=1), at(dz=3))
+        relay = [take("send", CHUNKS) for c in range(2)]
 
         def rows(s):
-            return pl.ds(s * size, size)
+            return pl.ds(pl.multiple_of(s * size, size), size)
 
         def start():
             @pl.when(mine)
             def _():
-                for copy in keep:
+                for copy in own:
                     copy.start()
 
             for s in range(CHUNKS):
                 for c, dy in ((0, 1), (1, 3)):
                     their = lax.rem(y + dy, 4) // 2
                     send(
+                        tag,
                         mine,
                         source.at[2 * c + their, rows(s)],
                         target.at[c, rows(s)],
@@ -158,47 +157,68 @@
                         at(dy=dy),
                     )
                     send(
+                        tag,
                         mine,
                         source.at[2 * c + yh, rows(s)],
                         target.at[c, rows(s)],
                         ring + c * CHUNKS + s,
-                        at(dz=1 if c == 0 else 3),
+                        up[c],
                     )
 
-        def step(s):
+        def onward(c, s):
+            here = target.at[c, rows(s)]
+            return pltpu.make_async_remote_copy(
+                src_ref=here,
+                dst_ref=here,
+                send_sem=send_sems.at[relay[c] + s],
+                recv_sem=recv_sems.at[ring + c * CHUNKS + s],
+                device_id=up[c],
+                device_id_type=MESH,
+            )
+
+        def step(t):
             for c in range(2):
+                s = t - hops[c]
+                live = jnp.logical_and(jnp.logical_not(mine), jnp.logical_and(s >= 0, s < CHUNKS))
                 here = target.at[c, rows(s)]
-                arrive(other, here, cross + c * CHUNKS + s)
-                arrive(dz != 0, here, ring + c * CHUNKS + s)
-                last = dz == (3 if c == 0 else 1)
-                send(
-                    jnp.logical_and(jnp.logical_not(mine), jnp.logical_not(last)),
-                    here,
-                    here,
-                    ring + c * CHUNKS + s,
-                    at(dz=1 if c == 0 else 3),
-                )
+                arrive(tag, jnp.logical_and(live, dz == 0), here, cross + c * CHUNKS + s)
+                arrive(tag, jnp.logical_and(live, dz != 0), here, ring + c * CHUNKS + s)
+                when_live(tag, jnp.logical_and(live, hops[c] != 3), lambda: onward(c, s).start())
 
         def finish():
             @pl.when(mine)
             def _():
-                for copy in keep:
+                for copy in own:
                     copy.wait()
 
+            for c in range(2):
+                cond = jnp.logical_and(jnp.logical_not(mine), hops[c] != 3)
+
+                def body():
+                    @pl.loop(0, CHUNKS)
+                    def _(s):
+                        onward(c, s).wait_send()
+
+                when_live(tag, cond, body)
+
         return start, step, finish
 
-    l_start, l_step, l_finish = exchange(low, lj)
+    def when_live(tag, cond, body):
+        when(cond, body)
+
+    l_start, l_step, l_finish = exchange("L", low, lj)
+    q_start, q_step, q_finish = exchange("Q", qi, qj)
+    STEPS = CHUNKS + 3
     l_start()
 
     dh[...], dl[...] = split(dinv[...])
-    arrive(col != 0, raw, raw_recv)
+    arrive("S", col != 0, raw, raw_recv)
     pl.when(col == 0)(lambda: own_raw.wait())
 
     for b in range(4):
         rows = jnp.concatenate([raw[b, :, t, :] for t in range(4)], axis=1)
         high, lo = split(rows)
         turned[b] = dot3(high, lo, dh[...], dl[...], NT)
-    turned[4] = turned[0]
 
     def slab(piece, count=5):
         return qi.at[pl.ds(0, count), pl.ds(pl.multiple_of(piece * part, part), part)]
@@ -207,25 +227,23 @@
     head2 = take("recv")
     pair = take("recv")
     partner = lax.rem(col + 8, PIECES)
-    send(None, turned.at[pl.ds(0, 4)], slab(col, 4), pair, at(dy=2))
+    send("Y", None, turned, slab(col, 4), pair, at(dy=2))
     my_head = qi.at[4, pl.ds(pl.multiple_of(col * part, part), part)]
     for r in range(8):
         if r:
-            send(row == 0, turned.at[4], my_head, head, (r, col))
-        send(row == 0, turned.at[4], my_head, head2, (r, partner))
-    keep4 = pltpu.make_async_copy(
-        turned.at[pl.ds(0, 4)], slab(col, 4), local_sems.at[take("local")]
-    )
+            send("R", row == 0, turned.at[0], my_head, head, (r, col))
+        send("R", row == 0, turned.at[0], my_head, head2, (r, partner))
+    keep4 = keep(turned, slab(col, 4))
     keep4.start()
-    keep1 = pltpu.make_async_copy(turned.at[4], my_head, local_sems.at[take("local")])
+    keep1 = keep(turned.at[0], my_head)
     pl.when(row == 0)(lambda: keep1.start())
 
-    for s in range(CHUNKS // 2):
-        l_step(s)
-
-    arrive(None, slab(partner, 4), pair)
-    arrive(row != 0, my_head, head)
-    arrive(None, qi.at[4, pl.ds(pl.multiple_of(partner * part, part), part)], head2)
+    for t in range(STEPS // 2):
+        l_step(t)
+
+    arrive("Y", None, slab(partner, 4), pair)
+    arrive("R", row != 0, my_head, head)
+    arrive("R", None, qi.at[4, pl.ds(pl.multiple_of(partner * part, part), part)], head2)
     keep4.wait()
     pl.when(row == 0)(lambda: keep1.wait())
 
@@ -236,41 +254,52 @@
     left = take("recv", 2)
     far = take("recv", 2)
     core = take("recv", 8)
-    both = (8 * 0 + 2 * x + k, 8 + 2 * x + k)
+    both = (2 * x + k, 8 + 2 * x + k)
     for h in range(2):
-        send(None, slab(both[h]), slab(both[h]), right + h, at(dx=1))
-        send(None, slab(both[h]), slab(both[h]), left + h, at(dx=3))
+        send("X", None, slab(both[h]), slab(both[h]), right + h, at(dx=1))
+        send("X", None, slab(both[h]), slab(both[h]), left + h, at(dx=3))
     for h in range(2):
-        send(None, slab(both[h]), slab(both[h]), core + h, at(dk=1))
-    for s in range(CHUNKS // 2, CHUNKS):
-        l_step(s)
+        send("K", None, slab(both[h]), slab(both[h]), core + h, at(dk=1))
+    for t in range(STEPS // 2, STEPS):
+        l_step(t)
     for h in (0, 1):
         from_left, from_right = near(both[h], 3), near(both[h], 1)
-        arrive(None, slab(from_left), right + h)
+        arrive("X", None, slab(from_left), right + h)
         if h == 0:
-            send(None, slab(from_left), slab(from_left), far, at(dx=1))
-        send(None, slab(from_left), slab(from_left), core + 2 + h, at(dk=1))
-        arrive(None, slab(from_right), left + h)
+            send("X", None, slab(from_left), slab(from_left), far, at(dx=1))
+        send("K", None, slab(from_left), slab(from_left), core + 2 + h, at(dk=1))
+        arrive("X", None, slab(from_right), left + h)
         if h == 1:
-            send(None, slab(from_right), slab(from_right), far + 1, at(dx=3))
-        send(None, slab(from_right), slab(from_right), core + 4 + h, at(dk=1))
+            send("X", None, slab(from_right), slab(from_right), far + 1, at(dx=3))
+        send("K", None, slab(from_right), slab(from_right), core + 4 + h, at(dk=1))
     for h in (0, 1):
         opposite = near(both[h], 2)
-        arrive(None, slab(opposite), far + h)
-        send(None, slab(opposite), slab(opposite), core + 6 + h, at(dk=1))
+        arrive("X", None, slab(opposite), far + h)
+        send("K", None, slab(opposite), slab(opposite), core + 6 + h, at(dk=1))
     for n, dx in enumerate((0, 3, 1, 2)):
         for h in range(2):
             theirs = 8 * h + 2 * lax.rem(x + dx, 4) + lax.rem(k + 1, 2)
-            arrive(None, slab(theirs), core + 2 * n + h)
+            arrive("K", None, slab(theirs), core + 2 * n + h)
 
     l_finish()
-    q_start, q_step, q_finish = exchange(qi, qj)
     q_start()
-    for s in range(CHUNKS):
-        q_step(s)
+    qi_save = keep(qi, qi_out)
+    qi_save.start()
+    lj_save = keep(lj, lj_out)
+    lj_save.start()
+
+    @pl.loop(0, STEPS)
+    def _(t):
+        q_step(t)
+
     q_finish()
+    qj_save = keep(qj, qj_out)
+    qj_save.start()
     for cond, body in open_sends:
         when(cond, body)
+    qi_save.wait()
+    lj_save.wait()
+    qj_save.wait()
     assert used["send"] <= send_sems.shape[0], used
     assert used["recv"] <= recv_sems.shape[0], used
     assert used["local"] <= local_sems.shape[0], used
@@ -279,7 +308,7 @@
 def gather(a, low, dinv):
     nb = dinv.shape[0]
     part = nb // PIECES
-    anywhere = pl.BlockSpec(memory_space=pltpu.HBM)
+    anywhere = pl.BlockSpec(memory_space=pl.ANY)
     return pl.pallas_call(
         gather_kernel,
         out_shape=(
@@ -291,15 +320,18 @@
         out_specs=(anywhere, anywhere, anywhere),
         scratch_shapes=[
             pltpu.VMEM((4, part, 4, 128), F32),
-            pltpu.VMEM((5, part, nb), F32),
+            pltpu.VMEM((4, part, nb), F32),
             pltpu.VMEM((nb, nb), BF),
             pltpu.VMEM((nb, nb), BF),
-            pltpu.SemaphoreType.DMA((160,)),
+            pltpu.VMEM((5, nb, nb), F32),
+            pltpu.VMEM((2, nb, nb), F32),
+            pltpu.VMEM((2, nb, nb), F32),
+            pltpu.SemaphoreType.DMA((190,)),
             pltpu.SemaphoreType.DMA((90,)),
-            pltpu.SemaphoreType.DMA((10,)),
+            pltpu.SemaphoreType.DMA((12,)),
         ],
         compiler_params=pltpu.CompilerParams(
-            collective_id=0, has_side_effects=True, vmem_limit_bytes=16 << 20
+            collective_id=0, has_side_effects=True, vmem_limit_bytes=60 << 20
         ),
         name="gather",
     )(a, low, dinv)

time: 363 us -> 163 us (0.45)
  the two profiles are of different devices: /device:TPU:28 before, /device:TPU:14 now
where the time goes in v2:
time: 163 us; the launch traced here: 162 us
  Pallas kernels  162 us (99%)
    pallas_call x1, Pallas kernels, gather(): pl.pallas_call(gather_kernel, out_shape=(jax.ShapeDtypeStruct((5, nb, nb)...  132 us
    pallas_call x1, Pallas kernels, update(): pl.pallas_call(update_kernel, grid=(4,), out_shape=jax.ShapeDtypeStruct(a...  30 us

profile of v2, /device:TPU:14, one launch (start us, length us, event | category | flops | bytes accessed | tf_op | source)
XLA Modules:
  0.0 162.4 jit_solution(7138692020707217239)
XLA Ops:
  0.0 132.4 %gather.1 = (f32[5,512,512]{2,1,0:T(8,128)}, f32[2,512,512]{2,1,0:T(8,128)}, f32[2,512,512]{2,1,0:T(8,128)}) custom-call(f32[4,512,2,4,128]{4,3,2,1,0:T(4,128)} %bitcast.4, f32[4,512,512]{2,1,0:T(8,128)} %bitcast.6, f32[512,512]{1,0:T(8,128)} %dinv.3), custom_call_target="tpu_custom_call" | custom-call | tf_op jit(solution)/shard_map/gather/pallas_call | solution.py:312
  132.4 30.0 %update.1 = f32[16384,128]{1,0:T(8,128)} custom-call(f32[16384,128]{1,0:T(8,128)} %bitcast.5, f32[5,512,512]{2,1,0:T(8,128)} %get-tuple-element.8.qi.r, f32[4,512,512]{2,1,0:T(8,128)} %bitcast.7, f32[2,512,512]{2,1,0:T(8,128)} %get-tuple-element.9.lj, f32[2,512,512]{2,1,0:T(8,128)} %get-tuple-element.10.qj, f32[5,512,512]{2,1,0:T(8,128)} %get-tuple-element.8.qi.r, ...), custom_call_target="tpu_custom_call" | custom-call | tf_op jit(solution)/shard_map/update/pallas_call | solution.py:412

commit v3 on v2

v3 whole, which is shorter than its diff:
```python
import functools

import jax
import jax.numpy as jnp
from jax import lax
from jax.experimental import pallas as pl
from jax.experimental.pallas import tpu as pltpu
from jax.sharding import PartitionSpec as P

F32, BF = jnp.float32, jnp.bfloat16
MESH = pl.DeviceIdType.MESH
NT = (((1,), (1,)), ((), ()))
NN = (((1,), (0,)), ((), ()))
PIECES = 16
CHUNKS = 8


def split(x):
    high = x.astype(BF)
    return high, (x - high.astype(F32)).astype(BF)


def dot3(ah, al, bh, bl, dims):
    dot = functools.partial(
        lax.dot_general, dimension_numbers=dims, preferred_element_type=F32
    )
    return dot(ah, bh) + dot(ah, bl) + dot(al, bh)


def gather_kernel(
    a, low, dinv, qi_out, lj_out, qj_out, raw, turned, dh, dl, qi, lj, qj, send_sems, recv_sems, local_sems
):
    row, col = lax.axis_index("row"), lax.axis_index("col")
    z, yl = row // 2, lax.rem(row, 2)
    yh, x, k = col // 8, lax.rem(col // 2, 4), lax.rem(col, 2)
    y = 2 * yh + yl
    nb = dinv.shape[0]
    part = nb // PIECES

    def at(dx=0, dy=0, dz=0, dk=0):
        nx, ny = lax.rem(x + dx + 4, 4), lax.rem(y + dy + 4, 4)
        nz, nk = lax.rem(z + dz + 4, 4), lax.rem(k + dk, 2)
        return (2 * nz + lax.rem(ny, 2), 8 * (ny // 2) + 2 * nx + nk)

    used = {"send": 0, "recv": 0, "local": 0}
    open_sends = []

    def take(kind, count=1):
        first = used[kind]
        used[kind] += count
        return first

    def when(cond, body):
        if cond is None:
            body()
        else:
            pl.when(cond)(body)

    def send(tag, cond, src, dst, recv, device):
        sem = take("send")

        def copy():
            return pltpu.make_async_remote_copy(
                src_ref=src,
                dst_ref=dst,
                send_sem=send_sems.at[sem],
                recv_sem=recv_sems.at[recv],
                device_id=device,
                device_id_type=MESH,
            )

        when(cond, lambda: copy().start())
        open_sends.append((cond, lambda: copy().wait_send()))

    def arrive(tag, cond, dst, recv):
        def body():
            pltpu.make_async_remote_copy(
                src_ref=dst,
                dst_ref=dst,
                send_sem=send_sems.at[0],
                recv_sem=recv_sems.at[recv],
                device_id=at(dk=1),
                device_id_type=MESH,
            ).wait_recv()

        when(cond, body)

    def keep(src, dst):
        return pltpu.make_async_copy(src, dst, local_sems.at[take("local")])

    barrier = pltpu.get_barrier_semaphore()

    def greet(cond, device):
        when(
            cond,
            lambda: pl.semaphore_signal(
                barrier, inc=1, device_id=device, device_id_type=MESH
            ),
        )

    neighbours = [at(dx=1), at(dx=3), at(dy=1), at(dy=3), at(dz=1), at(dz=3), at(dy=2), at(dk=1)]
    for device in neighbours:
        greet(None, device)
    greet(col != 0, (row, 0))
    greet(row != 0, (0, col))
    greet(None, (0, lax.rem(col + 8, PIECES)))
    expect = (
        len(neighbours)
        + jnp.where(col == 0, PIECES - 1, 0)
        + jnp.where(row == 0, 7 + 8, 0)
    )
    pl.semaphore_wait(barrier, expect)

    def place(eighth, upper, count=1):
        return pl.ds(pl.multiple_of((2 * eighth + upper) * part, part), count * part)

    raw_recv = take("recv")
    for piece in range(1, PIECES):
        send(
            "S",
            col == 0,
            a.at[:, place(piece % 8, piece // 8), 0],
            raw,
            raw_recv,
            (row, piece),
        )
    own_raw = keep(a.at[:, place(0, 0), 0], raw)
    pl.when(col == 0)(lambda: own_raw.start())

    dz = lax.rem(z - x + 4, 4)
    mine = jnp.logical_and(dz == 0, yl == k)
    relays = jnp.logical_not(mine)
    lag = jnp.where(yl == k, 0, 1)
    hops = (dz, lax.rem(4 - dz, 4))
    up = (at(dz=1), at(dz=3))

    def exchange(tag, source, target, chunks, rows):
        cross = take("recv", 2 * chunks)
        ring = take("recv", 2 * chunks)
        relay = take("send", 2 * chunks)

        def start(s):
            for c, dy in ((0, 1), (1, 3)):
                their = lax.rem(y + dy, 4) // 2
                send(
                    tag,
                    mine,
                    source.at[2 * c + yh, rows(s)],
                    target.at[c, rows(s)],
                    ring + c * chunks + s,
                    up[c],
                )
                send(
                    tag,
                    mine,
                    source.at[2 * c + their, rows(s)],
                    target.at[c, rows(s)],
                    cross + c * chunks + s,
                    at(dy=dy),
                )

        def onward(c, s):
            here = target.at[c, rows(s)]
            return pltpu.make_async_remote_copy(
                src_ref=here,
                dst_ref=here,
                send_sem=send_sems.at[relay + c * chunks + s],
                recv_sem=recv_sems.at[ring + c * chunks + s],
                device_id=up[c],
                device_id_type=MESH,
            )

        def step(t, group=1):
            for c in range(2):
                first = t - hops[c] - lag
                live = jnp.logical_and(
                    relays, jnp.logical_and(first >= 0, first < chunks // group)
                )
                for e in range(group):
                    s = first * group + e
                    here = target.at[c, rows(s)]
                    arrive(tag, jnp.logical_and(live, dz == 0), here, cross + c * chunks + s)
                    arrive(tag, jnp.logical_and(live, dz != 0), here, ring + c * chunks + s)
                    tagged(tag, jnp.logical_and(live, hops[c] != 3), lambda: onward(c, s).start())

        def finish():
            for c in range(2):

                def body():
                    @pl.loop(0, chunks)
                    def _(s):
                        onward(c, s).wait_send()

                tagged(tag, jnp.logical_and(relays, hops[c] != 3), body)

        return start, step, finish

    def tagged(tag, cond, body):
        when(cond, body)

    def own_blocks(source, target):
        return [keep(source.at[2 * c + yh], target.at[c]) for c in range(2)]

    size = nb // CHUNKS
    l_start, l_step, l_finish = exchange(
        "L", low, lj, CHUNKS, lambda s: pl.ds(pl.multiple_of(s * size, size), size)
    )
    l_own = own_blocks(low, lj)

    def slice_rows(s):
        group, other, e = s // 4, lax.rem(s // 2, 2), lax.rem(s, 2)
        ends = jnp.logical_or(group == 0, group == 3)
        upper = jnp.where(ends, e, group - 1)
        dx = jnp.where(group == 0, 0, jnp.where(group == 3, 2, 3 - 2 * e))
        return place(2 * lax.rem(x + dx, 4) + lax.rem(k + other, 2), upper)

    q_start, q_step, q_finish = exchange("Q", qi, qj, PIECES, slice_rows)
    q_own = own_blocks(qi, qj)

    @pl.when(mine)
    def _():
        for copy in l_own:
            copy.start()

    for s in range(CHUNKS):
        l_start(s)
    dh[...], dl[...] = split(dinv[...])
    for t in range(6):
        l_step(t)
    arrive("S", col != 0, raw, raw_recv)
    pl.when(col == 0)(lambda: own_raw.wait())

    rows = jnp.concatenate(
        [
            jnp.concatenate([raw[b, :, t, :] for t in range(4)], axis=1)
            for b in range(4)
        ],
        axis=0,
    )
    high, lo = split(rows)
    turned[...] = dot3(high, lo, dh[...], dl[...], NT).reshape(turned.shape)

    eighth = lax.rem(col, 8)
    across = lax.rem(col + 8, PIECES)

    def slab(here, count=1):
        return qi.at[pl.ds(0, 4), place(*here, count)]

    def head(here, count=1):
        return qi.at[4, place(*here, count)]

    def near(dx, dk=0):
        return 2 * lax.rem(x + dx, 4) + lax.rem(k + dk, 2)

    own, partner = (eighth, yh), (eighth, 1 - yh)
    pair = take("recv")
    send("Y", None, turned, slab(own), pair, at(dy=2))
    head_own, head_partner = take("recv"), take("recv")
    for r in range(8):
        if r:
            send("R", row == 0, turned.at[0], head(own), head_own, (r, col))
        send("R", row == 0, turned.at[0], head(own), head_partner, (r, across))
    keep_slab = keep(turned, slab(own))
    keep_slab.start()
    keep_head = keep(turned.at[0], head(own))
    pl.when(row == 0)(lambda: keep_head.start())
    for t in range(6, 9):
        l_step(t)
    keep_slab.wait()
    arrive("Y", None, slab(partner), pair)

    right, left, far = take("recv", 2), take("recv", 2), take("recv", 2)
    core_own, core_side, core_far = take("recv"), take("recv", 4), take("recv", 2)
    h_right, h_left, h_far, h_core = (
        take("recv"), take("recv"), take("recv"), take("recv", 4)
    )

    def pass_on(event):
        for s in (2 * event, 2 * event + 1):
            q_start(s)
        q_step(event, 2)

    for h in range(2):
        for target, dx in ((right, 1), (left, 3)):
            send("X", None, slab((eighth, h)), slab((eighth, h)), target + h, at(dx=dx))
    send("K", None, slab((eighth, 0), 2), slab((eighth, 0), 2), core_own, at(dk=1))
    pass_on(0)
    arrive("K", None, slab((near(0, 1), 0), 2), core_own)
    pass_on(1)
    for t in range(9, 12):
        l_step(t)
    for h in range(2):
        for n, (source, dx) in enumerate(((right, 3), (left, 1))):
            here = slab((near(dx), h))
            arrive("X", None, here, source + h)
            if n == h:
                send("X", None, here, here, far + h, at(dx=4 - dx))
            send("K", None, here, here, core_side + 2 * h + n, at(dk=1))
        pass_on(2 + 2 * h)
        if h == 1:
            pl.when(row == 0)(lambda: keep_head.wait())
            arrive("R", row != 0, head(own), head_own)
            arrive("R", None, head(partner), head_partner)
            mid = (eighth, 0)
            send("R", None, head(mid, 2), head(mid, 2), h_right, at(dx=1))
            send("R", None, head(mid, 2), head(mid, 2), h_left, at(dx=3))
            send("R", None, head(mid, 2), head(mid, 2), h_core, at(dk=1))
        for n, dx in enumerate((3, 1)):
            arrive("K", None, slab((near(dx, 1), h)), core_side + 2 * h + n)
        pass_on(3 + 2 * h)
    for h in range(2):
        here = slab((near(2), h))
        arrive("X", None, here, far + h)
        send("K", None, here, here, core_far + h, at(dk=1))
    pass_on(6)
    for n, (source, dx) in enumerate(((h_right, 3), (h_left, 1))):
        here = head((near(dx), 0), 2)
        arrive("R", None, here, source)
        if n == 0:
            send("R", None, here, here, h_far, at(dx=1))
        send("R", None, here, here, h_core + 1 + n, at(dk=1))
    for h in range(2):
        arrive("K", None, slab((near(2, 1), h)), core_far + h)
    pass_on(7)

    @pl.when(mine)
    def _():
        for copy in q_own:
            copy.start()

    q_step(8, 2)
    here = head((near(2), 0), 2)
    arrive("R", None, here, h_far)
    send("R", None, here, here, h_core + 3, at(dk=1))
    q_step(9, 2)
    for n, dx in enumerate((0, 3, 1, 2)):
        arrive("R", None, head((near(dx, 1), 0), 2), h_core + n)
    qi_save = keep(qi, qi_out)
    qi_save.start()
    q_step(10, 2)

    @pl.when(mine)
    def _():
        for copy in l_own + q_own:
            copy.wait()

    lj_save = keep(lj, lj_out)
    lj_save.start()
    q_step(11, 2)
    qj_save = keep(qj, qj_out)
    qj_save.start()
    l_finish()
    q_finish()
    for cond, body in open_sends:
        when(cond, body)
    qi_save.wait()
    lj_save.wait()
    qj_save.wait()
    assert used["send"] <= send_sems.shape[0], used
    assert used["recv"] <= recv_sems.shape[0], used
    assert used["local"] <= local_sems.shape[0], used


def gather(a, low, dinv):
    nb = dinv.shape[0]
    part = nb // PIECES
    anywhere = pl.BlockSpec(memory_space=pl.ANY)
    return pl.pallas_call(
        gather_kernel,
        out_shape=(
            jax.ShapeDtypeStruct((5, nb, nb), F32),
            jax.ShapeDtypeStruct((2, nb, nb), F32),
            jax.ShapeDtypeStruct((2, nb, nb), F32),
        ),
        in_specs=[anywhere, anywhere, pl.BlockSpec(memory_space=pltpu.VMEM)],
        out_specs=(anywhere, anywhere, anywhere),
        scratch_shapes=[
            pltpu.VMEM((4, part, 4, 128), F32),
            pltpu.VMEM((4, part, nb), F32),
            pltpu.VMEM((nb, nb), BF),
            pltpu.VMEM((nb, nb), BF),
            pltpu.VMEM((5, nb, nb), F32),
            pltpu.VMEM((2, nb, nb), F32),
            pltpu.VMEM((2, nb, nb), F32),
            pltpu.SemaphoreType.DMA((250,)),
            pltpu.SemaphoreType.DMA((140,)),
            pltpu.SemaphoreType.DMA((16,)),
        ],
        compiler_params=pltpu.CompilerParams(
            collective_id=0, has_side_effects=True, vmem_limit_bytes=60 << 20
        ),
        name="gather",
    )(a, low, dinv)


def update_kernel(a, qi, li, lj, qj, r, dinv, o, ys, xs, ch, cl, cf):
    b = pl.program_id(0)
    row, col = lax.axis_index("row"), lax.axis_index("col")
    nb = 512

    def halves(to, rows, at, values, low_twice):
        high, lo = split(values)
        for n in range(3):
            is_low = n == (1 if low_twice else 2)
            to[rows, pl.ds(2 * n * nb + at, nb)] = lo if is_low else high

    @pl.when(b == 0)
    def _():
        dh, dl = split(dinv[...])
        rh, rl = split(r[0])
        cf[...] = dot3(dh, dl, rh, rl, NN)
        ch[...], cl[...] = split(cf[...])
        sh, sl = split(0.5 * (cf[...] + cf[...].T))

        for c in range(2):
            rows = pl.ds(c * nb, nb)
            halves(ys, rows, 0, lj[c], True)
            g = qj[c] - dot3(ys[rows, :nb], ys[rows, pl.ds(2 * nb, nb)], sh, sl, NN)
            halves(ys, rows, nb, g, True)

    halves(xs, slice(None), 0, qi[0], False)
    halves(xs, slice(None), nb, li[0], False)

    @pl.loop(0, 2)
    def _(c):
        rows = pl.ds(pl.multiple_of(c * nb, nb), nb)
        top = jnp.logical_and(row == 0, b == 0)
        side = jnp.logical_and(col == 0, c == 0)

        def put(values):
            for t in range(4):
                o[pl.ds(c * 4 + t, nb, stride=8), :] = values(t)

        @pl.when(jnp.logical_not(jnp.logical_or(top, side)))
        def _():
            acc = lax.dot_general(xs[...], ys[rows, :], NT, preferred_element_type=F32)
            put(
                lambda t: a[pl.ds(c * 4 + t, nb, stride=8), :]
                - acc[:, t * 128 : (t + 1) * 128]
            )

        @pl.when(jnp.logical_and(side, jnp.logical_not(top)))
        def _():
            fin = qi[0] - dot3(
                xs[:, pl.ds(nb, nb)], xs[:, pl.ds(5 * nb, nb)], ch[...], cl[...], NN
            )
            put(lambda t: fin[:, t * 128 : (t + 1) * 128])

        @pl.when(jnp.logical_and(top, jnp.logical_not(side)))
        def _():
            fin = qj[c] - dot3(
                ys[rows, :nb], ys[rows, pl.ds(2 * nb, nb)], ch[...], cl[...], NN
            )
            fin = fin.T
            put(lambda t: fin[:, t * 128 : (t + 1) * 128])

        @pl.when(jnp.logical_and(top, side))
        def _():
            put(lambda t: cf[:, t * 128 : (t + 1) * 128])


def update(a, qi, li, lj, qj, dinv):
    nb = dinv.shape[0]
    pairs = pl.BlockSpec((2, nb, nb), lambda b: (0, 0, 0))
    block = pl.BlockSpec((1, nb, nb), lambda b: (b, 0, 0))
    linear = pl.BlockSpec((8 * nb, 128), lambda b: (b, 0))
    return pl.pallas_call(
        update_kernel,
        grid=(4,),
        out_shape=jax.ShapeDtypeStruct(a.shape, F32),
        in_specs=[
            linear,
            block,
            block,
            pairs,
            pairs,
            pl.BlockSpec((1, nb, nb), lambda b: (4, 0, 0)),
            pl.BlockSpec((nb, nb), lambda b: (0, 0)),
        ],
        out_specs=linear,
        scratch_shapes=[
            pltpu.VMEM((2 * nb, 6 * nb), BF),
            pltpu.VMEM((nb, 6 * nb), BF),
            pltpu.VMEM((nb, nb), BF),
            pltpu.VMEM((nb, nb), BF),
            pltpu.VMEM((nb, nb), F32),
        ],
        compiler_params=pltpu.CompilerParams(vmem_limit_bytes=56 << 20),
        name="update",
    )(a, qi, li, lj, qj, qi, dinv)


def body(stiffness, lower_panel, diag_inverse):
    shape = stiffness.shape
    tiles = stiffness.reshape(4, 512, 2, 4, 128)
    rows = stiffness.reshape(16384, 128)
    low = lower_panel[:, 0]
    qi, lj, qj = gather(tiles, low, diag_inverse)
    out = update(rows, qi, low, lj, qj, diag_inverse)
    return out.reshape(shape)


def solution(mesh):
    in_specs = (P(None, "row", None, None, "col", None), P(None, "row", None, None), P())
    out_specs = P(None, "row", None, None, "col", None)
    return jax.shard_map(body, mesh=mesh, in_specs=in_specs, out_specs=out_specs, check_vma=False)
```

time: 163 us -> 121 us (0.74)
  the two profiles are of different devices: /device:TPU:14 before, /device:TPU:28 now
where the time goes in v3:
time: 121 us; the launch traced here: 120 us
  Pallas kernels  120 us (99%)
    pallas_call x1, Pallas kernels, gather(): pl.pallas_call(gather_kernel, out_shape=(jax.ShapeDtypeStruct((5, nb, nb)...  93.4 us
    pallas_call x1, Pallas kernels, update(): pl.pallas_call(update_kernel, grid=(4,), out_shape=jax.ShapeDtypeStruct(a...  26.1 us

profile of v3, /device:TPU:28, one launch (start us, length us, event | category | flops | bytes accessed | tf_op | source)
XLA Modules:
  0.0 119.6 jit_solution(201977973318057232)
XLA Ops:
  0.0 93.4 %gather.1 = (f32[5,512,512]{2,1,0:T(8,128)}, f32[2,512,512]{2,1,0:T(8,128)}, f32[2,512,512]{2,1,0:T(8,128)}) custom-call(f32[4,512,2,4,128]{4,3,2,1,0:T(4,128)} %bitcast.4, f32[4,512,512]{2,1,0:T(8,128)} %bitcast.6, f32[512,512]{1,0:T(8,128)} %dinv.3), custom_call_target="tpu_custom_call" | custom-call | tf_op jit(solution)/shard_map/gather/pallas_call | solution.py:368
  93.4 26.1 %update.1 = f32[16384,128]{1,0:T(8,128)} custom-call(f32[16384,128]{1,0:T(8,128)} %bitcast.5, f32[5,512,512]{2,1,0:T(8,128)} %get-tuple-element.8.qi.r, f32[4,512,512]{2,1,0:T(8,128)} %bitcast.7, f32[2,512,512]{2,1,0:T(8,128)} %get-tuple-element.9.lj, f32[2,512,512]{2,1,0:T(8,128)} %get-tuple-element.10.qj, f32[5,512,512]{2,1,0:T(8,128)} %get-tuple-element.8.qi.r, ...), custom_call_target="tpu_custom_call" | custom-call | tf_op jit(solution)/shard_map/update/pallas_call | solution.py:467

commit v4 on v3

v4 whole, which is shorter than its diff:
```python
import functools

import jax
import jax.numpy as jnp
from jax import lax
from jax.experimental import pallas as pl
from jax.experimental.pallas import tpu as pltpu
from jax.sharding import PartitionSpec as P

F32, BF = jnp.float32, jnp.bfloat16
MESH = pl.DeviceIdType.MESH
NT = (((1,), (1,)), ((), ()))
NN = (((1,), (0,)), ((), ()))
PIECES = 16
CHUNKS = 8


def split(x):
    high = x.astype(BF)
    return high, (x - high.astype(F32)).astype(BF)


def dot3(ah, al, bh, bl, dims):
    dot = functools.partial(
        lax.dot_general, dimension_numbers=dims, preferred_element_type=F32
    )
    return dot(ah, bh) + dot(ah, bl) + dot(al, bh)


def gather_kernel(
    a, low, dinv, xh_out, xl_out, yh_out, yl_out, c_out,
    raw, turned, dh, dl, li, qi, lj, qj, xh, xl, yh, yl, cf, sh, sl, send_sems, recv_sems, local_sems,
):
    row, col = lax.axis_index("row"), lax.axis_index("col")
    z, ylo = row // 2, lax.rem(row, 2)
    yhi, x, k = col // 8, lax.rem(col // 2, 4), lax.rem(col, 2)
    y = 2 * yhi + ylo
    nb = dinv.shape[0]
    part = nb // PIECES

    def at(dx=0, dy=0, dz=0, dk=0):
        nx, ny = lax.rem(x + dx + 4, 4), lax.rem(y + dy + 4, 4)
        nz, nk = lax.rem(z + dz + 4, 4), lax.rem(k + dk, 2)
        return (2 * nz + lax.rem(ny, 2), 8 * (ny // 2) + 2 * nx + nk)

    used = {"send": 0, "recv": 0, "local": 0}
    open_sends = []

    def take(kind, count=1):
        first = used[kind]
        used[kind] += count
        return first

    def when(cond, body):
        if cond is None:
            body()
        else:
            pl.when(cond)(body)

    def tagged(tag, cond, body):
        when(cond, body)

    def send(tag, cond, src, dst, recv, device):
        sem = take("send")

        def copy():
            return pltpu.make_async_remote_copy(
                src_ref=src,
                dst_ref=dst,
                send_sem=send_sems.at[sem],
                recv_sem=recv_sems.at[recv],
                device_id=device,
                device_id_type=MESH,
            )

        when(cond, lambda: copy().start())
        open_sends.append((cond, lambda: copy().wait_send()))

    def arrive(tag, cond, dst, recv):
        def body():
            pltpu.make_async_remote_copy(
                src_ref=dst,
                dst_ref=dst,
                send_sem=send_sems.at[0],
                recv_sem=recv_sems.at[recv],
                device_id=at(dk=1),
                device_id_type=MESH,
            ).wait_recv()

        when(cond, body)

    def keep(src, dst):
        return pltpu.make_async_copy(src, dst, local_sems.at[take("local")])

    load_low = keep(low, li)
    load_low.start()
    barrier = pltpu.get_barrier_semaphore()

    def greet(cond, device):
        when(
            cond,
            lambda: pl.semaphore_signal(
                barrier, inc=1, device_id=device, device_id_type=MESH
            ),
        )

    neighbours = [at(dx=1), at(dx=3), at(dy=1), at(dy=3), at(dz=1), at(dz=3), at(dy=2), at(dk=1)]
    greet(col != 0, (row, 0))
    for device in neighbours:
        greet(None, device)
    greet(row != 0, (0, col))
    expect = (
        len(neighbours)
        + jnp.where(col == 0, PIECES - 1, 0)
        + jnp.where(row == 0, 7, 0)
    )
    pl.semaphore_wait(barrier, expect)

    def place(eighth, upper, count=1):
        return pl.ds(pl.multiple_of((2 * eighth + upper) * part, part), count * part)

    raw_recv = take("recv")
    for piece in range(1, PIECES):
        send(
            "S",
            col == 0,
            a.at[:, place(piece % 8, piece // 8), 0],
            raw,
            raw_recv,
            (row, piece),
        )
    own_raw = keep(a.at[:, place(0, 0), 0], raw)
    pl.when(col == 0)(lambda: own_raw.start())

    dz = lax.rem(z - x + 4, 4)
    mine = jnp.logical_and(dz == 0, ylo == k)
    relays = jnp.logical_not(mine)
    lag = jnp.where(ylo == k, 0, 1)
    hops = (dz, lax.rem(4 - dz, 4))
    up = (at(dz=1), at(dz=3))
    order = tuple(
        jnp.where(ylo == k, yhi, lax.rem(y + dy, 4) // 2) for dy in (3, 1)
    )

    def exchange(tag, source, target, chunks, rows):
        cross = take("recv", 2 * chunks)
        ring = take("recv", 2 * chunks)
        relay = take("send", 2 * chunks)

        def start(s):
            for c, dy in ((0, 1), (1, 3)):
                their = lax.rem(y + dy, 4) // 2
                here = rows(s, yhi)
                send(tag, mine, source.at[2 * c + yhi, here], target.at[c, here], ring + c * chunks + s, up[c])
                send(tag, mine, source.at[2 * c + their, here], target.at[c, here], cross + c * chunks + s, at(dy=dy))

        def onward(c, s):
            here = target.at[c, rows(s, order[c])]
            return pltpu.make_async_remote_copy(
                src_ref=here,
                dst_ref=here,
                send_sem=send_sems.at[relay + c * chunks + s],
                recv_sem=recv_sems.at[ring + c * chunks + s],
                device_id=up[c],
                device_id_type=MESH,
            )

        def step(t, group=1):
            for c in range(2):
                first = t - hops[c] - lag
                live = jnp.logical_and(
                    relays, jnp.logical_and(first >= 0, first < chunks // group)
                )
                for e in range(group):
                    s = first * group + e
                    here = target.at[c, rows(s, order[c])]
                    arrive(tag, jnp.logical_and(live, dz == 0), here, cross + c * chunks + s)
                    arrive(tag, jnp.logical_and(live, dz != 0), here, ring + c * chunks + s)
                    tagged(tag, jnp.logical_and(live, hops[c] != 3), lambda: onward(c, s).start())

        def finish():
            for c in range(2):

                def body():
                    @pl.loop(0, chunks)
                    def _(s):
                        onward(c, s).wait_send()

                tagged(tag, jnp.logical_and(relays, hops[c] != 3), body)

        return start, step, finish

    def own_blocks(source, target):
        return [keep(source.at[2 * c + yhi], target.at[c]) for c in range(2)]

    size = nb // CHUNKS
    l_start, l_step, l_finish = exchange(
        "L", low, lj, CHUNKS, lambda s, half: pl.ds(pl.multiple_of(s * size, size), size)
    )
    l_own = own_blocks(low, lj)

    def slice_rows(s, half):
        group, other, e = s // 4, lax.rem(s // 2, 2), lax.rem(s, 2)
        ends = jnp.logical_or(group == 0, group == 3)
        second = jnp.where(ends, e, group - 1)
        upper = jnp.where(second == 0, half, 1 - half)
        dx = jnp.where(group == 0, 0, jnp.where(group == 3, 2, 3 - 2 * e))
        return place(2 * lax.rem(x + dx, 4) + lax.rem(k + other, 2), upper)

    q_start, q_step, q_finish = exchange("Q", qi, qj, PIECES, slice_rows)
    q_own = own_blocks(qi, qj)

    def spread(source, target, half, count=8):
        size = nb // count

        @pl.loop(0, count)
        def _(n):
            rows = pl.ds(pl.multiple_of(n * size, size), size)
            cols = pl.ds(half * nb, nb)
            target[0][rows, cols], target[1][rows, cols] = split(source[rows, :])

    @pl.when(mine)
    def _():
        for copy in l_own:
            copy.start()

    for s in range(CHUNKS):
        l_start(s)
    dh[...], dl[...] = split(dinv[...])
    l_step(0)
    load_low.wait()
    for b in range(4):
        spread(li.at[b], (xh.at[b], xl.at[b]), 1)
        l_step(1 + b)
    arrive("S", col != 0, raw, raw_recv)
    pl.when(col == 0)(lambda: own_raw.wait())

    rows = jnp.concatenate(
        [
            jnp.concatenate([raw[b, :, t, :] for t in range(4)], axis=1)
            for b in range(4)
        ],
        axis=0,
    )
    high, lo = split(rows)
    turned[...] = dot3(high, lo, dh[...], dl[...], NT).reshape(turned.shape)

    def near(dx, dk=0):
        return 2 * lax.rem(x + dx, 4) + lax.rem(k + dk, 2)

    halves = (yhi, 1 - yhi)

    def slab(eighth, upper):
        return qi.at[pl.ds(0, 4), place(eighth, upper)]

    def head(eighth, upper, count=1):
        return qi.at[4, place(eighth, upper, count)]

    def into_halves(eighth, upper):
        here = place(eighth, upper)

        @pl.loop(0, 4)
        def _(b):
            xh[b, here, pl.ds(0, nb)], xl[b, here, pl.ds(0, nb)] = split(qi[b, here, :])

    right, left, far, core = take("recv", 2), take("recv", 2), take("recv", 2), take("recv", 8)
    pair, head_own, head_partner = take("recv"), take("recv"), take("recv")
    h_right, h_left, h_far, h_core = take("recv"), take("recv"), take("recv"), take("recv", 4)

    def side(n, src):
        here = slab(near(0), halves[n])
        send("X", None, src, here, right + n, at(dx=1))
        send("X", None, src, here, left + n, at(dx=3))
        send("K", None, src, here, core + n, at(dk=1))

    def pass_on(event):
        for s in (2 * event, 2 * event + 1):
            q_start(s)
        q_step(event, 2)

    send("Y", None, turned, slab(near(0), yhi), pair, at(dy=2))
    side(0, turned)
    my_head = head(near(0), yhi)
    for r in range(1, 8):
        send("R", row == 0, turned.at[0], my_head, head_own, (r, col))
    keep_slab = keep(turned, slab(near(0), yhi))
    keep_slab.start()
    keep_head = keep(turned.at[0], my_head)
    pl.when(row == 0)(lambda: keep_head.start())
    keep_slab.wait()
    q_start(0)
    arrive("Y", None, slab(near(0), 1 - yhi), pair)
    side(1, slab(near(0), 1 - yhi))
    q_start(1)
    pl.when(row == 0)(lambda: keep_head.wait())
    arrive("R", row != 0, my_head, head_own)
    send("R", None, my_head, my_head, head_partner, at(dy=2))
    q_step(0, 2)
    l_step(5)
    for n in range(2):
        arrive("K", None, slab(near(0, 1), halves[n]), core + n)
    pass_on(1)
    l_step(6)
    for n in range(2):
        into_halves(near(0), n)
        into_halves(near(0, 1), n)
    for h in range(2):
        for n, (source, dx) in enumerate(((right, 3), (left, 1))):
            here = slab(near(dx), halves[h])
            arrive("X", None, here, source + h)
            if n == h:
                send("X", None, here, here, far + h, at(dx=4 - dx))
            send("K", None, here, here, core + 2 + 2 * h + n, at(dk=1))
        pass_on(2 + 2 * h)
        if h == 0:
            arrive("R", None, head(near(0), 1 - yhi), head_partner)
            mid = head(near(0), 0, 2)
            send("R", None, mid, mid, h_right, at(dx=1))
            send("R", None, mid, mid, h_left, at(dx=3))
            send("R", None, mid, mid, h_core, at(dk=1))
        else:
            for n, (source, dx) in enumerate(((h_right, 3), (h_left, 1))):
                here = head(near(dx), 0, 2)
                arrive("R", None, here, source)
                if n == 0:
                    send("R", None, here, here, h_far, at(dx=1))
                send("R", None, here, here, h_core + 1 + n, at(dk=1))
        l_step(7 + 2 * h)
        for n, dx in enumerate((3, 1)):
            arrive("K", None, slab(near(dx, 1), halves[h]), core + 2 + 2 * h + n)
        pass_on(3 + 2 * h)
        l_step(8 + 2 * h)
        for dx in (3, 1):
            into_halves(near(dx), halves[h])
            into_halves(near(dx, 1), halves[h])
    for h in range(2):
        here = slab(near(2), halves[h])
        arrive("X", None, here, far + h)
        send("K", None, here, here, core + 6 + h, at(dk=1))
    pass_on(6)
    here = head(near(2), 0, 2)
    arrive("R", None, here, h_far)
    send("R", None, here, here, h_core + 3, at(dk=1))
    l_step(11)
    for h in range(2):
        arrive("K", None, slab(near(2, 1), halves[h]), core + 6 + h)
    pass_on(7)

    @pl.when(mine)
    def _():
        for copy in q_own:
            copy.start()

    saves = []

    def save(pairs):
        for src, dst in pairs:
            one = keep(src, dst)
            one.start()
            saves.append(one)

    for n in range(2):
        into_halves(near(2), n)
        into_halves(near(2, 1), n)
    save([(xh, xh_out), (xl, xl_out)])

    @pl.when(mine)
    def _():
        for copy in l_own:
            copy.wait()

    for c in range(2):
        spread(lj.at[c], (yh.at[c], yl.at[c]), 0)
    q_step(8, 2)
    for n, dx in enumerate((0, 3, 1, 2)):
        arrive("R", None, head(near(dx, 1), 0, 2), h_core + n)

    rh, rl = split(qi[4])
    cf[...] = dot3(dh[...], dl[...], rh, rl, NN)
    sh[...], sl[...] = split(0.5 * (cf[...] + cf[...].T))
    save([(cf, c_out)])
    q_step(9, 2)
    l_finish()
    lj[0] = dot3(yh[0, :, :nb], yl[0, :, :nb], sh[...], sl[...], NN)
    q_step(10, 2)
    lj[1] = dot3(yh[1, :, :nb], yl[1, :, :nb], sh[...], sl[...], NN)
    q_step(11, 2)

    @pl.when(mine)
    def _():
        for copy in q_own:
            copy.wait()

    for c in range(2):

        @pl.loop(0, 8)
        def _(n):
            here = pl.ds(pl.multiple_of(n * (nb // 8), nb // 8), nb // 8)
            cols = pl.ds(nb, nb)
            yh[c, here, cols], yl[c, here, cols] = split(qj[c, here, :] - lj[c, here, :])

        save([(yh.at[c], yh_out.at[c]), (yl.at[c], yl_out.at[c])])
    q_finish()
    for cond, body in open_sends:
        when(cond, body)
    for one in saves:
        one.wait()
    assert used["send"] <= send_sems.shape[0], used
    assert used["recv"] <= recv_sems.shape[0], used
    assert used["local"] <= local_sems.shape[0], used


def gather(a, low, dinv):
    nb = dinv.shape[0]
    part = nb // PIECES
    anywhere = pl.BlockSpec(memory_space=pl.ANY)
    return pl.pallas_call(
        gather_kernel,
        out_shape=(
            jax.ShapeDtypeStruct((4, nb, 2 * nb), BF),
            jax.ShapeDtypeStruct((4, nb, 2 * nb), BF),
            jax.ShapeDtypeStruct((2, nb, 2 * nb), BF),
            jax.ShapeDtypeStruct((2, nb, 2 * nb), BF),
            jax.ShapeDtypeStruct((nb, nb), F32),
        ),
        in_specs=[anywhere, anywhere, pl.BlockSpec(memory_space=pltpu.VMEM)],
        out_specs=(anywhere,) * 5,
        scratch_shapes=[
            pltpu.VMEM((4, part, 4, 128), F32),
            pltpu.VMEM((4, part, nb), F32),
            pltpu.VMEM((nb, nb), BF),
            pltpu.VMEM((nb, nb), BF),
            pltpu.VMEM((4, nb, nb), F32),
            pltpu.VMEM((5, nb, nb), F32),
            pltpu.VMEM((2, nb, nb), F32),
            pltpu.VMEM((2, nb, nb), F32),
            pltpu.VMEM((4, nb, 2 * nb), BF),
            pltpu.VMEM((4, nb, 2 * nb), BF),
            pltpu.VMEM((2, nb, 2 * nb), BF),
            pltpu.VMEM((2, nb, 2 * nb), BF),
            pltpu.VMEM((nb, nb), F32),
            pltpu.VMEM((nb, nb), BF),
            pltpu.VMEM((nb, nb), BF),
            pltpu.SemaphoreType.DMA((280,)),
            pltpu.SemaphoreType.DMA((140,)),
            pltpu.SemaphoreType.DMA((32,)),
        ],
        compiler_params=pltpu.CompilerParams(
            collective_id=0, has_side_effects=True, vmem_limit_bytes=60 << 20
        ),
        name="gather",
    )(a, low, dinv)


def update_kernel(a, xh, xl, yh, yl, cf, o, ch, cl, sh, sl):
    b = pl.program_id(0)
    row, col = lax.axis_index("row"), lax.axis_index("col")
    nb = cf.shape[0]
    edge = jnp.logical_or(row == 0, col == 0)

    @pl.when(jnp.logical_and(b == 0, edge))
    def _():
        ch[...], cl[...] = split(cf[...])
        sh[...], sl[...] = split(0.5 * (cf[...] - cf[...].T))

    dot = functools.partial(
        lax.dot_general, dimension_numbers=NT, preferred_element_type=F32
    )

    @pl.loop(0, 2)
    def _(c):
        top = jnp.logical_and(row == 0, b == 0)
        side = jnp.logical_and(col == 0, c == 0)

        def put(values):
            for t in range(4):
                o[pl.ds(c * 4 + t, nb, stride=8), :] = values(t)

        @pl.when(jnp.logical_not(jnp.logical_or(top, side)))
        def _():
            acc = dot(xh[0], yh[c]) + dot(xh[0], yl[c]) + dot(xl[0], yh[c])
            put(
                lambda t: a[pl.ds(c * 4 + t, nb, stride=8), :]
                - acc[:, t * 128 : (t + 1) * 128]
            )

        @pl.when(jnp.logical_and(side, jnp.logical_not(top)))
        def _():
            fin = dot3(xh[0, :, nb:], xl[0, :, nb:], ch[...], cl[...], NN)
            fin = (xh[0, :, :nb].astype(F32) + xl[0, :, :nb].astype(F32)) - fin
            put(lambda t: fin[:, t * 128 : (t + 1) * 128])

        @pl.when(jnp.logical_and(top, jnp.logical_not(side)))
        def _():
            fin = dot3(yh[c, :, :nb], yl[c, :, :nb], sh[...], sl[...], NN)
            fin = (yh[c, :, nb:].astype(F32) + yl[c, :, nb:].astype(F32)) - fin
            fin = fin.T
            put(lambda t: fin[:, t * 128 : (t + 1) * 128])

        @pl.when(jnp.logical_and(top, side))
        def _():
            put(lambda t: cf[:, t * 128 : (t + 1) * 128])


def update(a, xh, xl, yh, yl, cf):
    nb = cf.shape[0]
    pairs = pl.BlockSpec((2, nb, 2 * nb), lambda b: (0, 0, 0))
    block = pl.BlockSpec((1, nb, 2 * nb), lambda b: (b, 0, 0))
    linear = pl.BlockSpec((8 * nb, 128), lambda b: (b, 0))
    return pl.pallas_call(
        update_kernel,
        grid=(4,),
        out_shape=jax.ShapeDtypeStruct(a.shape, F32),
        in_specs=[linear, block, block, pairs, pairs, pl.BlockSpec((nb, nb), lambda b: (0, 0))],
        out_specs=linear,
        scratch_shapes=[pltpu.VMEM((nb, nb), BF)] * 4,
        compiler_params=pltpu.CompilerParams(vmem_limit_bytes=56 << 20),
        name="update",
    )(a, xh, xl, yh, yl, cf)


def body(stiffness, lower_panel, diag_inverse):
    tiles = stiffness.reshape(4, 512, 2, 4, 128)
    rows = stiffness.reshape(16384, 128)
    out = update(rows, *gather(tiles, lower_panel[:, 0], diag_inverse))
    return out.reshape(stiffness.shape)


def solution(mesh):
    in_specs = (P(None, "row", None, None, "col", None), P(None, "row", None, None), P())
    out_specs = P(None, "row", None, None, "col", None)
    return jax.shard_map(body, mesh=mesh, in_specs=in_specs, out_specs=out_specs, check_vma=False)
```

time: 121 us -> 123 us (1.017)
  the two profiles are of different devices: /device:TPU:28 before, /device:TPU:108 now
where the time goes in v4:
time: 123 us
  Pallas kernels  123 us (100%)
    pallas_call x1, Pallas kernels, gather(): pl.pallas_call(gather_kernel, out_shape=(jax.ShapeDtypeStruct((4, nb, 2 *...  101 us
    pallas_call x1, Pallas kernels, update(): pl.pallas_call(update_kernel, grid=(4,), out_shape=jax.ShapeDtypeStruct(a...  21.5 us

profile of v4, /device:TPU:108, one launch (start us, length us, event | category | flops | bytes accessed | tf_op | source)
XLA Modules:
  0.0 122.9 jit_solution(14298614536581605249)
XLA Ops:
  0.0 101.4 %gather.1 = (bf16[4,512,1024]{2,1,0:T(8,128)(2,1)}, bf16[4,512,1024]{2,1,0:T(8,128)(2,1)}, bf16[2,512,1024]{2,1,0:T(8,128)(2,1)}, bf16[2,512,1024]{2,1,0:T(8,128)(2,1)}, f32[512,512]{1,0:T(8,128)}) custom-call(f32[4,512,2,4,128]{4,3,2,1,0:T(4,128)} %bitcast.4, f32[4,512,512]{2,1,0:T(8,128)} %bitcast.6, f32[512,512]{1,0:T(8,128)} %dinv.1), custom_call_target="tpu_custom_call" | custom-call | tf_op jit(solution)/shard_map/gather/pallas_call | solution.py:417
  101.4 21.5 %update.1 = f32[16384,128]{1,0:T(8,128)} custom-call(f32[16384,128]{1,0:T(8,128)} %bitcast.5, bf16[4,512,1024]{2,1,0:T(8,128)(2,1)} %get-tuple-element.10.xh, bf16[4,512,1024]{2,1,0:T(8,128)(2,1)} %get-tuple-element.11.xl, bf16[2,512,1024]{2,1,0:T(8,128)(2,1)} %get-tuple-element.12.yh, bf16[2,512,1024]{2,1,0:T(8,128)(2,1)} %get-tuple-element.13.yl, ...), custom_call_target="tpu_custom_call" | custom-call | tf_op jit(solution)/shard_map/update/pallas_call | solution.py:510

commit v5 on v4

--- a/solution.py
+++ b/solution.py
@@ -133,81 +133,108 @@
     pl.when(col == 0)(lambda: own_raw.start())
 
     dz = lax.rem(z - x + 4, 4)
-    mine = jnp.logical_and(dz == 0, ylo == k)
-    relays = jnp.logical_not(mine)
-    lag = jnp.where(ylo == k, 0, 1)
-    hops = (dz, lax.rem(4 - dz, 4))
+    chain = ylo == k
+    mine = jnp.logical_and(dz == 0, chain)
+    relays = jnp.logical_and(dz != 0, chain)
+    hops = tuple(jnp.where(h == 3, 1, h) for h in (dz, lax.rem(4 - dz, 4)))
+    passes = (dz == 1, dz == 3)
     up = (at(dz=1), at(dz=3))
-    order = tuple(
-        jnp.where(ylo == k, yhi, lax.rem(y + dy, 4) // 2) for dy in (3, 1)
-    )
+    beside = at(dy=jnp.where(ylo == 0, 1, 3))
 
     def exchange(tag, source, target, chunks, rows):
         cross = take("recv", 2 * chunks)
         ring = take("recv", 2 * chunks)
-        relay = take("send", 2 * chunks)
-
-        def start(s):
-            for c, dy in ((0, 1), (1, 3)):
-                their = lax.rem(y + dy, 4) // 2
-                here = rows(s, yhi)
-                send(tag, mine, source.at[2 * c + yhi, here], target.at[c, here], ring + c * chunks + s, up[c])
-                send(tag, mine, source.at[2 * c + their, here], target.at[c, here], cross + c * chunks + s, at(dy=dy))
-
-        def onward(c, s):
-            here = target.at[c, rows(s, order[c])]
+        to_ring = take("send", 2 * chunks)
+        to_cross = take("send", 2 * chunks)
+        to_back = take("send", 2 * chunks)
+
+        def move(src, here, sends, recvs, n, device):
             return pltpu.make_async_remote_copy(
-                src_ref=here,
+                src_ref=src,
                 dst_ref=here,
-                send_sem=send_sems.at[relay + c * chunks + s],
-                recv_sem=recv_sems.at[ring + c * chunks + s],
-                device_id=up[c],
+                send_sem=send_sems.at[sends + n],
+                recv_sem=recv_sems.at[recvs + n],
+                device_id=device,
                 device_id_type=MESH,
             )
 
+        def both_ways(c, s, src, here):
+            n = c * chunks + s
+            return (
+                move(src, here, to_ring, ring, n, up[c]),
+                move(src, here, to_cross, cross, n, beside),
+            )
+
+        def start(s):
+            @pl.when(mine)
+            def _():
+                for c in range(2):
+                    here = rows(s)
+                    src, dst = source.at[2 * c + yhi, here], target.at[c, here]
+                    for one in both_ways(c, s, src, dst):
+                        one.start()
+                    move(src, dst, to_back, ring, c * chunks + s, up[1 - c]).start()
+
         def step(t, group=1):
             for c in range(2):
-                first = t - hops[c] - lag
+                first = t - hops[c]
                 live = jnp.logical_and(
                     relays, jnp.logical_and(first >= 0, first < chunks // group)
                 )
                 for e in range(group):
                     s = first * group + e
-                    here = target.at[c, rows(s, order[c])]
-                    arrive(tag, jnp.logical_and(live, dz == 0), here, cross + c * chunks + s)
-                    arrive(tag, jnp.logical_and(live, dz != 0), here, ring + c * chunks + s)
-                    tagged(tag, jnp.logical_and(live, hops[c] != 3), lambda: onward(c, s).start())
+                    here = target.at[c, rows(s)]
+
+                    @pl.when(live)
+                    def _():
+                        arrive(tag, None, here, ring + c * chunks + s)
+                        onward, over = both_ways(c, s, here, here)
+                        pl.when(passes[c])(lambda: onward.start())
+                        over.start()
+
+        def take_over():
+            @pl.when(jnp.logical_not(chain))
+            def _():
+                @pl.loop(0, chunks)
+                def _(s):
+                    for c in range(2):
+                        arrive(tag, None, target.at[c, rows(s)], cross + c * chunks + s)
 
         def finish():
-            for c in range(2):
-
-                def body():
-                    @pl.loop(0, chunks)
-                    def _(s):
-                        onward(c, s).wait_send()
-
-                tagged(tag, jnp.logical_and(relays, hops[c] != 3), body)
-
-        return start, step, finish
+            @pl.when(chain)
+            def _():
+                @pl.loop(0, chunks)
+                def _(s):
+                    for c in range(2):
+                        here = target.at[c, rows(s)]
+                        onward, over = both_ways(c, s, here, here)
+                        n = c * chunks + s
+                        pl.when(jnp.logical_or(mine, passes[c]))(lambda: onward.wait_send())
+                        over.wait_send()
+                        pl.when(mine)(
+                            lambda: move(here, here, to_back, ring, n, up[1 - c]).wait_send()
+                        )
+
+        return start, step, take_over, finish
 
     def own_blocks(source, target):
         return [keep(source.at[2 * c + yhi], target.at[c]) for c in range(2)]
 
     size = nb // CHUNKS
-    l_start, l_step, l_finish = exchange(
-        "L", low, lj, CHUNKS, lambda s, half: pl.ds(pl.multiple_of(s * size, size), size)
+    l_start, l_step, l_take_over, l_finish = exchange(
+        "L", low, lj, CHUNKS, lambda s: pl.ds(pl.multiple_of(s * size, size), size)
     )
     l_own = own_blocks(low, lj)
 
-    def slice_rows(s, half):
+    def slice_rows(s):
         group, other, e = s // 4, lax.rem(s // 2, 2), lax.rem(s, 2)
         ends = jnp.logical_or(group == 0, group == 3)
         second = jnp.where(ends, e, group - 1)
-        upper = jnp.where(second == 0, half, 1 - half)
+        upper = jnp.where(second == 0, yhi, 1 - yhi)
         dx = jnp.where(group == 0, 0, jnp.where(group == 3, 2, 3 - 2 * e))
         return place(2 * lax.rem(x + dx, 4) + lax.rem(k + other, 2), upper)
 
-    q_start, q_step, q_finish = exchange("Q", qi, qj, PIECES, slice_rows)
+    q_start, q_step, q_take_over, q_finish = exchange("Q", qi, qj, PIECES, slice_rows)
     q_own = own_blocks(qi, qj)
 
     def spread(source, target, half, count=8):
@@ -232,6 +259,7 @@
     for b in range(4):
         spread(li.at[b], (xh.at[b], xl.at[b]), 1)
         l_step(1 + b)
+    l_step(5)
     arrive("S", col != 0, raw, raw_recv)
     pl.when(col == 0)(lambda: own_raw.wait())
 
@@ -287,8 +315,10 @@
     keep_slab.start()
     keep_head = keep(turned.at[0], my_head)
     pl.when(row == 0)(lambda: keep_head.start())
+    l_step(6)
     keep_slab.wait()
     q_start(0)
+    l_step(7)
     arrive("Y", None, slab(near(0), 1 - yhi), pair)
     side(1, slab(near(0), 1 - yhi))
     q_start(1)
@@ -296,11 +326,11 @@
     arrive("R", row != 0, my_head, head_own)
     send("R", None, my_head, my_head, head_partner, at(dy=2))
     q_step(0, 2)
-    l_step(5)
+    l_step(8)
     for n in range(2):
         arrive("K", None, slab(near(0, 1), halves[n]), core + n)
     pass_on(1)
-    l_step(6)
+    l_step(9)
     for n in range(2):
         into_halves(near(0), n)
         into_halves(near(0, 1), n)
@@ -325,11 +355,19 @@
                 if n == 0:
                     send("R", None, here, here, h_far, at(dx=1))
                 send("R", None, here, here, h_core + 1 + n, at(dk=1))
-        l_step(7 + 2 * h)
         for n, dx in enumerate((3, 1)):
             arrive("K", None, slab(near(dx, 1), halves[h]), core + 2 + 2 * h + n)
         pass_on(3 + 2 * h)
-        l_step(8 + 2 * h)
+        if h == 0:
+
+            @pl.when(mine)
+            def _():
+                for copy in l_own:
+                    copy.wait()
+
+            l_take_over()
+            for c in range(2):
+                spread(lj.at[c], (yh.at[c], yl.at[c]), 0)
         for dx in (3, 1):
             into_halves(near(dx), halves[h])
             into_halves(near(dx, 1), halves[h])
@@ -341,7 +379,6 @@
     here = head(near(2), 0, 2)
     arrive("R", None, here, h_far)
     send("R", None, here, here, h_core + 3, at(dk=1))
-    l_step(11)
     for h in range(2):
         arrive("K", None, slab(near(2, 1), halves[h]), core + 6 + h)
     pass_on(7)
@@ -359,19 +396,12 @@
             one.start()
             saves.append(one)
 
+    q_step(8, 2)
     for n in range(2):
         into_halves(near(2), n)
         into_halves(near(2, 1), n)
     save([(xh, xh_out), (xl, xl_out)])
-
-    @pl.when(mine)
-    def _():
-        for copy in l_own:
-            copy.wait()
-
-    for c in range(2):
-        spread(lj.at[c], (yh.at[c], yl.at[c]), 0)
-    q_step(8, 2)
+    q_step(9, 2)
     for n, dx in enumerate((0, 3, 1, 2)):
         arrive("R", None, head(near(dx, 1), 0, 2), h_core + n)
 
@@ -379,12 +409,10 @@
     cf[...] = dot3(dh[...], dl[...], rh, rl, NN)
     sh[...], sl[...] = split(0.5 * (cf[...] + cf[...].T))
     save([(cf, c_out)])
-    q_step(9, 2)
     l_finish()
-    lj[0] = dot3(yh[0, :, :nb], yl[0, :, :nb], sh[...], sl[...], NN)
-    q_step(10, 2)
-    lj[1] = dot3(yh[1, :, :nb], yl[1, :, :nb], sh[...], sl[...], NN)
-    q_step(11, 2)
+    for c in range(2):
+        lj[c] = dot3(yh[c, :, :nb], yl[c, :, :nb], sh[...], sl[...], NN)
+    q_take_over()
 
     @pl.when(mine)
     def _():
@@ -441,7 +469,7 @@
             pltpu.VMEM((nb, nb), F32),
             pltpu.VMEM((nb, nb), BF),
             pltpu.VMEM((nb, nb), BF),
-            pltpu.SemaphoreType.DMA((280,)),
+            pltpu.SemaphoreType.DMA((300,)),
             pltpu.SemaphoreType.DMA((140,)),
             pltpu.SemaphoreType.DMA((32,)),
         ],

time: 123 us -> 110 us (0.89)
  the two profiles are of different devices: /device:TPU:108 before, /device:TPU:28 now
where the time goes in v5:
time: 110 us
  Pallas kernels  110 us (100%)
    pallas_call x1, Pallas kernels, gather(): pl.pallas_call(gather_kernel, out_shape=(jax.ShapeDtypeStruct((4, nb, 2 *...  88.7 us
    pallas_call x1, Pallas kernels, update(): pl.pallas_call(update_kernel, grid=(4,), out_shape=jax.ShapeDtypeStruct(a...  21.5 us

profile of v5, /device:TPU:28, one launch (start us, length us, event | category | flops | bytes accessed | tf_op | source)
XLA Modules:
  0.0 110.2 jit_solution(9125326917511457899)
XLA Ops:
  0.0 88.7 %gather.1 = (bf16[4,512,1024]{2,1,0:T(8,128)(2,1)}, bf16[4,512,1024]{2,1,0:T(8,128)(2,1)}, bf16[2,512,1024]{2,1,0:T(8,128)(2,1)}, bf16[2,512,1024]{2,1,0:T(8,128)(2,1)}, f32[512,512]{1,0:T(8,128)}) custom-call(f32[4,512,2,4,128]{4,3,2,1,0:T(4,128)} %bitcast.4, f32[4,512,512]{2,1,0:T(8,128)} %bitcast.6, f32[512,512]{1,0:T(8,128)} %dinv.1), custom_call_target="tpu_custom_call" | custom-call | tf_op jit(solution)/shard_map/gather/pallas_call | solution.py:445
  88.7 21.5 %update.1 = f32[16384,128]{1,0:T(8,128)} custom-call(f32[16384,128]{1,0:T(8,128)} %bitcast.5, bf16[4,512,1024]{2,1,0:T(8,128)(2,1)} %get-tuple-element.10.xh, bf16[4,512,1024]{2,1,0:T(8,128)(2,1)} %get-tuple-element.11.xl, bf16[2,512,1024]{2,1,0:T(8,128)(2,1)} %get-tuple-element.12.yh, bf16[2,512,1024]{2,1,0:T(8,128)(2,1)} %get-tuple-element.13.yl, ...), custom_call_target="tpu_custom_call" | custom-call | tf_op jit(solution)/shard_map/update/pallas_call | solution.py:538

commit v6 on v5

--- a/solution.py
+++ b/solution.py
@@ -28,8 +28,9 @@
 
 
 def gather_kernel(
-    a, low, dinv, xh_out, xl_out, yh_out, yl_out, c_out,
-    raw, turned, dh, dl, li, qi, lj, qj, xh, xl, yh, yl, cf, sh, sl, send_sems, recv_sems, local_sems,
+    a, blocks, low, dinv, a_out, lih_out, lil_out, gh_out, gl_out,
+    raw, turned, dh, dl, li, qi, lj, qj, blk, qh, ql, lih, lil, ljh, ljl, gh, gl, cf, sh, sl,
+    send_sems, recv_sems, local_sems,
 ):
     row, col = lax.axis_index("row"), lax.axis_index("col")
     z, ylo = row // 2, lax.rem(row, 2)
@@ -94,6 +95,8 @@
 
     load_low = keep(low, li)
     load_low.start()
+    load_blocks = keep(blocks, blk)
+    load_blocks.start()
     barrier = pltpu.get_barrier_semaphore()
 
     def greet(cond, device):
@@ -120,7 +123,7 @@
         return pl.ds(pl.multiple_of((2 * eighth + upper) * part, part), count * part)
 
     raw_recv = take("recv")
-    for piece in range(1, PIECES):
+    for piece in (12, 10, 13, 11, 4, 2, 5, 3, 14, 8, 15, 9, 6, 1, 7):
         send(
             "S",
             col == 0,
@@ -237,14 +240,13 @@
     q_start, q_step, q_take_over, q_finish = exchange("Q", qi, qj, PIECES, slice_rows)
     q_own = own_blocks(qi, qj)
 
-    def spread(source, target, half, count=8):
+    def spread(source, high, low_part, count=8):
         size = nb // count
 
         @pl.loop(0, count)
         def _(n):
             rows = pl.ds(pl.multiple_of(n * size, size), size)
-            cols = pl.ds(half * nb, nb)
-            target[0][rows, cols], target[1][rows, cols] = split(source[rows, :])
+            high[rows, :], low_part[rows, :] = split(source[rows, :])
 
     @pl.when(mine)
     def _():
@@ -257,7 +259,7 @@
     l_step(0)
     load_low.wait()
     for b in range(4):
-        spread(li.at[b], (xh.at[b], xl.at[b]), 1)
+        spread(li.at[b], lih.at[b], lil.at[b])
         l_step(1 + b)
     l_step(5)
     arrive("S", col != 0, raw, raw_recv)
@@ -289,7 +291,7 @@
 
         @pl.loop(0, 4)
         def _(b):
-            xh[b, here, pl.ds(0, nb)], xl[b, here, pl.ds(0, nb)] = split(qi[b, here, :])
+            qh[b, here, :], ql[b, here, :] = split(qi[b, here, :])
 
     right, left, far, core = take("recv", 2), take("recv", 2), take("recv", 2), take("recv", 8)
     pair, head_own, head_partner = take("recv"), take("recv"), take("recv")
@@ -367,7 +369,7 @@
 
             l_take_over()
             for c in range(2):
-                spread(lj.at[c], (yh.at[c], yl.at[c]), 0)
+                spread(lj.at[c], ljh.at[c], ljl.at[c])
         for dx in (3, 1):
             into_halves(near(dx), halves[h])
             into_halves(near(dx, 1), halves[h])
@@ -396,11 +398,43 @@
             one.start()
             saves.append(one)
 
+    @pl.when(row == 0)
+    def _():
+        lih[0] = jnp.zeros((nb, nb), BF)
+        lil[0] = jnp.zeros((nb, nb), BF)
+
+    save([(lih, lih_out), (lil, lil_out)])
+
+    def put(b, c, values):
+        for t in range(4):
+            here = pl.ds(b * 8 * nb + c * 4 + t, nb, stride=8)
+            blk[here, :] = values(here, t)
+
+    def first_half(b):
+        @pl.loop(0, 2)
+        def _(c):
+            side = jnp.logical_and(col == 0, c == 0)
+
+            @pl.when(side)
+            def _():
+                put(b, c, lambda here, t: qi[b, :, t * 128 : (t + 1) * 128])
+
+            @pl.when(jnp.logical_not(jnp.logical_or(side, row + b == 0)))
+            def _():
+                acc = dot3(qh[b], ql[b], ljh[c], ljl[c], NT)
+                put(b, c, lambda here, t: blk[here, :] - acc[:, t * 128 : (t + 1) * 128])
+
+    def save_block(b):
+        here = pl.ds(b * 8 * nb, 8 * nb)
+        save([(blk.at[here], a_out.at[here])])
+
     q_step(8, 2)
     for n in range(2):
         into_halves(near(2), n)
         into_halves(near(2, 1), n)
-    save([(xh, xh_out), (xl, xl_out)])
+    load_blocks.wait()
+    first_half(3)
+    save_block(3)
     q_step(9, 2)
     for n, dx in enumerate((0, 3, 1, 2)):
         arrive("R", None, head(near(dx, 1), 0, 2), h_core + n)
@@ -408,10 +442,13 @@
     rh, rl = split(qi[4])
     cf[...] = dot3(dh[...], dl[...], rh, rl, NN)
     sh[...], sl[...] = split(0.5 * (cf[...] + cf[...].T))
-    save([(cf, c_out)])
+    for b in (2, 1):
+        first_half(b)
+        save_block(b)
     l_finish()
     for c in range(2):
-        lj[c] = dot3(yh[c, :, :nb], yl[c, :, :nb], sh[...], sl[...], NN)
+        lj[c] = dot3(ljh[c], ljl[c], sh[...], sl[...], NN)
+    first_half(0)
     q_take_over()
 
     @pl.when(mine)
@@ -424,10 +461,30 @@
         @pl.loop(0, 8)
         def _(n):
             here = pl.ds(pl.multiple_of(n * (nb // 8), nb // 8), nb // 8)
-            cols = pl.ds(nb, nb)
-            yh[c, here, cols], yl[c, here, cols] = split(qj[c, here, :] - lj[c, here, :])
-
-        save([(yh.at[c], yh_out.at[c]), (yl.at[c], yl_out.at[c])])
+            gh[c, here, :], gl[c, here, :] = split(qj[c, here, :] - lj[c, here, :])
+
+        if c == 0:
+
+            @pl.when(col == 0)
+            def _():
+                gh[0], gl[0] = split(cf[...].T)
+
+        save([(gh.at[c], gh_out.at[c]), (gl.at[c], gl_out.at[c])])
+
+    @pl.when(row == 0)
+    def _():
+        sh[...], sl[...] = split(cf[...])
+
+        @pl.loop(0, 2)
+        def _(c):
+            fin = (qj[c] - dot3(ljh[c], ljl[c], sh[...], sl[...], NN)).T
+            put(0, c, lambda here, t: fin[:, t * 128 : (t + 1) * 128])
+
+        @pl.when(col == 0)
+        def _():
+            put(0, 0, lambda here, t: cf[:, t * 128 : (t + 1) * 128])
+
+    save_block(0)
     q_finish()
     for cond, body in open_sends:
         when(cond, body)
@@ -438,20 +495,20 @@
     assert used["local"] <= local_sems.shape[0], used
 
 
-def gather(a, low, dinv):
+def gather(a, blocks, low, dinv):
     nb = dinv.shape[0]
     part = nb // PIECES
     anywhere = pl.BlockSpec(memory_space=pl.ANY)
     return pl.pallas_call(
         gather_kernel,
         out_shape=(
-            jax.ShapeDtypeStruct((4, nb, 2 * nb), BF),
-            jax.ShapeDtypeStruct((4, nb, 2 * nb), BF),
-            jax.ShapeDtypeStruct((2, nb, 2 * nb), BF),
-            jax.ShapeDtypeStruct((2, nb, 2 * nb), BF),
-            jax.ShapeDtypeStruct((nb, nb), F32),
+            jax.ShapeDtypeStruct(blocks.shape, F32),
+            jax.ShapeDtypeStruct((4, nb, nb), BF),
+            jax.ShapeDtypeStruct((4, nb, nb), BF),
+            jax.ShapeDtypeStruct((2, nb, nb), BF),
+            jax.ShapeDtypeStruct((2, nb, nb), BF),
         ),
-        in_specs=[anywhere, anywhere, pl.BlockSpec(memory_space=pltpu.VMEM)],
+        in_specs=[anywhere, anywhere, anywhere, pl.BlockSpec(memory_space=pltpu.VMEM)],
         out_specs=(anywhere,) * 5,
         scratch_shapes=[
             pltpu.VMEM((4, part, 4, 128), F32),
@@ -462,14 +519,19 @@
             pltpu.VMEM((5, nb, nb), F32),
             pltpu.VMEM((2, nb, nb), F32),
             pltpu.VMEM((2, nb, nb), F32),
-            pltpu.VMEM((4, nb, 2 * nb), BF),
-            pltpu.VMEM((4, nb, 2 * nb), BF),
-            pltpu.VMEM((2, nb, 2 * nb), BF),
-            pltpu.VMEM((2, nb, 2 * nb), BF),
+            pltpu.VMEM(blocks.shape, F32),
+            pltpu.VMEM((4, nb, nb), BF),
+            pltpu.VMEM((4, nb, nb), BF),
+            pltpu.VMEM((4, nb, nb), BF),
+            pltpu.VMEM((4, nb, nb), BF),
+            pltpu.VMEM((2, nb, nb), BF),
+            pltpu.VMEM((2, nb, nb), BF),
+            pltpu.VMEM((2, nb, nb), BF),
+            pltpu.VMEM((2, nb, nb), BF),
             pltpu.VMEM((nb, nb), F32),
             pltpu.VMEM((nb, nb), BF),
             pltpu.VMEM((nb, nb), BF),
-            pltpu.SemaphoreType.DMA((300,)),
+            pltpu.SemaphoreType.DMA((280,)),
             pltpu.SemaphoreType.DMA((140,)),
             pltpu.SemaphoreType.DMA((32,)),
         ],
@@ -477,80 +539,40 @@
             collective_id=0, has_side_effects=True, vmem_limit_bytes=60 << 20
         ),
         name="gather",
-    )(a, low, dinv)
-
-
-def update_kernel(a, xh, xl, yh, yl, cf, o, ch, cl, sh, sl):
-    b = pl.program_id(0)
-    row, col = lax.axis_index("row"), lax.axis_index("col")
-    nb = cf.shape[0]
-    edge = jnp.logical_or(row == 0, col == 0)
-
-    @pl.when(jnp.logical_and(b == 0, edge))
-    def _():
-        ch[...], cl[...] = split(cf[...])
-        sh[...], sl[...] = split(0.5 * (cf[...] - cf[...].T))
-
-    dot = functools.partial(
-        lax.dot_general, dimension_numbers=NT, preferred_element_type=F32
-    )
+    )(a, blocks, low, dinv)
+
+
+def update_kernel(a, lh, ll, gh, gl, o):
+    nb = lh.shape[1]
 
     @pl.loop(0, 2)
     def _(c):
-        top = jnp.logical_and(row == 0, b == 0)
-        side = jnp.logical_and(col == 0, c == 0)
-
-        def put(values):
-            for t in range(4):
-                o[pl.ds(c * 4 + t, nb, stride=8), :] = values(t)
-
-        @pl.when(jnp.logical_not(jnp.logical_or(top, side)))
-        def _():
-            acc = dot(xh[0], yh[c]) + dot(xh[0], yl[c]) + dot(xl[0], yh[c])
-            put(
-                lambda t: a[pl.ds(c * 4 + t, nb, stride=8), :]
-                - acc[:, t * 128 : (t + 1) * 128]
-            )
-
-        @pl.when(jnp.logical_and(side, jnp.logical_not(top)))
-        def _():
-            fin = dot3(xh[0, :, nb:], xl[0, :, nb:], ch[...], cl[...], NN)
-            fin = (xh[0, :, :nb].astype(F32) + xl[0, :, :nb].astype(F32)) - fin
-            put(lambda t: fin[:, t * 128 : (t + 1) * 128])
-
-        @pl.when(jnp.logical_and(top, jnp.logical_not(side)))
-        def _():
-            fin = dot3(yh[c, :, :nb], yl[c, :, :nb], sh[...], sl[...], NN)
-            fin = (yh[c, :, nb:].astype(F32) + yl[c, :, nb:].astype(F32)) - fin
-            fin = fin.T
-            put(lambda t: fin[:, t * 128 : (t + 1) * 128])
-
-        @pl.when(jnp.logical_and(top, side))
-        def _():
-            put(lambda t: cf[:, t * 128 : (t + 1) * 128])
-
-
-def update(a, xh, xl, yh, yl, cf):
-    nb = cf.shape[0]
-    pairs = pl.BlockSpec((2, nb, 2 * nb), lambda b: (0, 0, 0))
-    block = pl.BlockSpec((1, nb, 2 * nb), lambda b: (b, 0, 0))
+        acc = dot3(lh[0], ll[0], gh[c], gl[c], NT)
+        for t in range(4):
+            here = pl.ds(c * 4 + t, nb, stride=8)
+            o[here, :] = a[here, :] - acc[:, t * 128 : (t + 1) * 128]
+
+
+def update(a, lh, ll, gh, gl):
+    nb = lh.shape[1]
+    pairs = pl.BlockSpec((2, nb, nb), lambda b: (0, 0, 0))
+    block = pl.BlockSpec((1, nb, nb), lambda b: (b, 0, 0))
     linear = pl.BlockSpec((8 * nb, 128), lambda b: (b, 0))
     return pl.pallas_call(
         update_kernel,
         grid=(4,),
         out_shape=jax.ShapeDtypeStruct(a.shape, F32),
-        in_specs=[linear, block, block, pairs, pairs, pl.BlockSpec((nb, nb), lambda b: (0, 0))],
+        in_specs=[linear, block, block, pairs, pairs],
         out_specs=linear,
-        scratch_shapes=[pltpu.VMEM((nb, nb), BF)] * 4,
         compiler_params=pltpu.CompilerParams(vmem_limit_bytes=56 << 20),
         name="update",
-    )(a, xh, xl, yh, yl, cf)
+    )(a, lh, ll, gh, gl)
 
 
 def body(stiffness, lower_panel, diag_inverse):
     tiles = stiffness.reshape(4, 512, 2, 4, 128)
     rows = stiffness.reshape(16384, 128)
-    out = update(rows, *gather(tiles, lower_panel[:, 0], diag_inverse))
+    out = update(*gather(tiles, rows, lower_panel[:, 0], diag_inverse))
     return out.reshape(stiffness.shape)
 
 

time: 110 us -> 104 us (0.945)
  the two profiles are of different devices: /device:TPU:28 before, /device:TPU:22 now
where the time goes in v6:
time: 104 us; the launch traced here: 103 us
  Pallas kernels  103 us (99%)
    pallas_call x1, Pallas kernels, gather(): pl.pallas_call(gather_kernel, out_shape=(jax.ShapeDtypeStruct(blocks.shap...  89.7 us
    pallas_call x1, Pallas kernels, update(): pl.pallas_call(update_kernel, grid=(4,), out_shape=jax.ShapeDtypeStruct(a...  13.7 us

profile of v6, /device:TPU:22, one launch (start us, length us, event | category | flops | bytes accessed | tf_op | source)
XLA Modules:
  0.0 103.4 jit_solution(6825016794441125847)
XLA Ops:
  0.0 89.7 %gather.1 = (f32[16384,128]{1,0:T(8,128)}, bf16[4,512,512]{2,1,0:T(8,128)(2,1)}, bf16[4,512,512]{2,1,0:T(8,128)(2,1)}, bf16[2,512,512]{2,1,0:T(8,128)(2,1)}, bf16[2,512,512]{2,1,0:T(8,128)(2,1)}) custom-call(f32[4,512,2,4,128]{4,3,2,1,0:T(4,128)} %bitcast.4, f32[16384,128]{1,0:T(8,128)} %bitcast.5, f32[4,512,512]{2,1,0:T(8,128)} %bitcast.6, f32[512,512]{1,0:T(8,128)} %dinv.1), custom_call_target="tpu_custom_call" | custom-call | tf_op jit(solution)/shard_map/gather/pallas_call | solution.py:502
  89.7 13.7 %update.1 = f32[16384,128]{1,0:T(8,128)} custom-call(f32[16384,128]{1,0:T(8,128)} %get-tuple-element.10.a, bf16[4,512,512]{2,1,0:T(8,128)(2,1)} %get-tuple-element.11.lh, bf16[4,512,512]{2,1,0:T(8,128)(2,1)} %get-tuple-element.12.ll, bf16[2,512,512]{2,1,0:T(8,128)(2,1)} %get-tuple-element.13.gh, bf16[2,512,512]{2,1,0:T(8,128)(2,1)} %get-tuple-element.14.gl), custom_call_target="tpu_custom_call" | custom-call | tf_op jit(solution)/shard_map/update/pallas_call | solution.py:561

commit v7 on v6

--- a/solution.py
+++ b/solution.py
@@ -292,6 +292,34 @@
         @pl.loop(0, 4)
         def _(b):
             qh[b, here, :], ql[b, here, :] = split(qi[b, here, :])
+
+    def first_half(eighth):
+        pair_rows = place(eighth, 0, 2)
+        count = 2 * part
+
+        @pl.loop(0, 2)
+        def _(c):
+            side = jnp.logical_and(col == 0, c == 0)
+
+            def put_rows(values):
+                for b in range(4):
+                    for t in range(4):
+                        start = b * 8 * nb + 16 * eighth * part + c * 4 + t
+                        here = pl.ds(start, count, stride=8)
+                        blk[here, :] = values(here, b, slice(t * 128, (t + 1) * 128))
+
+            @pl.when(side)
+            def _():
+                put_rows(lambda here, b, cols: qi[b, pair_rows, cols])
+
+            @pl.when(jnp.logical_not(side))
+            def _():
+                high = qh[:, pair_rows, :].reshape(4 * count, nb)
+                rest = ql[:, pair_rows, :].reshape(4 * count, nb)
+                acc = dot3(high, rest, ljh[c], ljl[c], NT)
+                put_rows(
+                    lambda here, b, cols: blk[here, :] - acc[b * count : (b + 1) * count, cols]
+                )
 
     right, left, far, core = take("recv", 2), take("recv", 2), take("recv", 2), take("recv", 8)
     pair, head_own, head_partner = take("recv"), take("recv"), take("recv")
@@ -370,9 +398,17 @@
             l_take_over()
             for c in range(2):
                 spread(lj.at[c], ljh.at[c], ljl.at[c])
+            load_blocks.wait()
         for dx in (3, 1):
             into_halves(near(dx), halves[h])
             into_halves(near(dx, 1), halves[h])
+        if h == 0:
+            first_half(near(0))
+            first_half(near(0, 1))
+        else:
+            for dx in (3, 1):
+                first_half(near(dx))
+                first_half(near(dx, 1))
     for h in range(2):
         here = slab(near(2), halves[h])
         arrive("X", None, here, far + h)
@@ -410,20 +446,6 @@
             here = pl.ds(b * 8 * nb + c * 4 + t, nb, stride=8)
             blk[here, :] = values(here, t)
 
-    def first_half(b):
-        @pl.loop(0, 2)
-        def _(c):
-            side = jnp.logical_and(col == 0, c == 0)
-
-            @pl.when(side)
-            def _():
-                put(b, c, lambda here, t: qi[b, :, t * 128 : (t + 1) * 128])
-
-            @pl.when(jnp.logical_not(jnp.logical_or(side, row + b == 0)))
-            def _():
-                acc = dot3(qh[b], ql[b], ljh[c], ljl[c], NT)
-                put(b, c, lambda here, t: blk[here, :] - acc[:, t * 128 : (t + 1) * 128])
-
     def save_block(b):
         here = pl.ds(b * 8 * nb, 8 * nb)
         save([(blk.at[here], a_out.at[here])])
@@ -432,9 +454,10 @@
     for n in range(2):
         into_halves(near(2), n)
         into_halves(near(2, 1), n)
-    load_blocks.wait()
-    first_half(3)
-    save_block(3)
+    first_half(near(2))
+    first_half(near(2, 1))
+    for b in range(1, 4):
+        save_block(b)
     q_step(9, 2)
     for n, dx in enumerate((0, 3, 1, 2)):
         arrive("R", None, head(near(dx, 1), 0, 2), h_core + n)
@@ -442,13 +465,9 @@
     rh, rl = split(qi[4])
     cf[...] = dot3(dh[...], dl[...], rh, rl, NN)
     sh[...], sl[...] = split(0.5 * (cf[...] + cf[...].T))
-    for b in (2, 1):
-        first_half(b)
-        save_block(b)
     l_finish()
     for c in range(2):
         lj[c] = dot3(ljh[c], ljl[c], sh[...], sl[...], NN)
-    first_half(0)
     q_take_over()
 
     @pl.when(mine)
@@ -545,11 +564,12 @@
 def update_kernel(a, lh, ll, gh, gl, o):
     nb = lh.shape[1]
 
-    @pl.loop(0, 2)
-    def _(c):
-        acc = dot3(lh[0], ll[0], gh[c], gl[c], NT)
-        for t in range(4):
-            here = pl.ds(c * 4 + t, nb, stride=8)
+    half = nb // 2
+    for n in range(4):
+        cols = pl.ds(n % 2 * half, half)
+        acc = dot3(lh[0], ll[0], gh[n // 2, cols], gl[n // 2, cols], NT)
+        for t in range(2):
+            here = pl.ds(n * 2 + t, nb, stride=8)
             o[here, :] = a[here, :] - acc[:, t * 128 : (t + 1) * 128]
 
 

time: 104 us -> 102 us (0.981)
  the two profiles are of different devices: /device:TPU:22 before, /device:TPU:28 now
where the time goes in v7:
time: 102 us; the launch traced here: 100 us
  Pallas kernels  100 us (98%)
    pallas_call x1, Pallas kernels, gather(): pl.pallas_call(gather_kernel, out_shape=(jax.ShapeDtypeStruct(blocks.shap...  87.1 us
    pallas_call x1, Pallas kernels, update(): pl.pallas_call(update_kernel, grid=(4,), out_shape=jax.ShapeDtypeStruct(a...  13.2 us

profile of v7, /device:TPU:28, one launch (start us, length us, event | category | flops | bytes accessed | tf_op | source)
XLA Modules:
  0.0 100.3 jit_solution(4703878374347071845)
XLA Ops:
  0.0 87.1 %gather.1 = (f32[16384,128]{1,0:T(8,128)}, bf16[4,512,512]{2,1,0:T(8,128)(2,1)}, bf16[4,512,512]{2,1,0:T(8,128)(2,1)}, bf16[2,512,512]{2,1,0:T(8,128)(2,1)}, bf16[2,512,512]{2,1,0:T(8,128)(2,1)}) custom-call(f32[4,512,2,4,128]{4,3,2,1,0:T(4,128)} %bitcast.4, f32[16384,128]{1,0:T(8,128)} %bitcast.5, f32[4,512,512]{2,1,0:T(8,128)} %bitcast.6, f32[512,512]{1,0:T(8,128)} %dinv.1), custom_call_target="tpu_custom_call" | custom-call | tf_op jit(solution)/shard_map/gather/pallas_call | solution.py:521
  87.1 13.2 %update.1 = f32[16384,128]{1,0:T(8,128)} custom-call(f32[16384,128]{1,0:T(8,128)} %get-tuple-element.10.a, bf16[4,512,512]{2,1,0:T(8,128)(2,1)} %get-tuple-element.11.lh, bf16[4,512,512]{2,1,0:T(8,128)(2,1)} %get-tuple-element.12.ll, bf16[2,512,512]{2,1,0:T(8,128)(2,1)} %get-tuple-element.13.gh, bf16[2,512,512]{2,1,0:T(8,128)(2,1)} %get-tuple-element.14.gl), custom_call_target="tpu_custom_call" | custom-call | tf_op jit(solution)/shard_map/update/pallas_call | solution.py:581

commit v8 on v7

--- a/solution.py
+++ b/solution.py
@@ -28,8 +28,8 @@
 
 
 def gather_kernel(
-    a, blocks, low, dinv, a_out, lih_out, lil_out, gh_out, gl_out,
-    raw, turned, dh, dl, li, qi, lj, qj, blk, qh, ql, lih, lil, ljh, ljl, gh, gl, cf, sh, sl,
+    a, blocks, low, dinv_in, a_out, lih_out, lil_out, gh_out, gl_out,
+    dinv, raw, turned, dh, dl, li, qi, lj, qj, blk, qh, ql, lih, lil, ljh, ljl, gh, gl, cf, sh, sl,
     send_sems, recv_sems, local_sems,
 ):
     row, col = lax.axis_index("row"), lax.axis_index("col")
@@ -93,6 +93,8 @@
     def keep(src, dst):
         return pltpu.make_async_copy(src, dst, local_sems.at[take("local")])
 
+    load_dinv = keep(dinv_in, dinv)
+    load_dinv.start()
     load_low = keep(low, li)
     load_low.start()
     load_blocks = keep(blocks, blk)
@@ -255,6 +257,7 @@
 
     for s in range(CHUNKS):
         l_start(s)
+    load_dinv.wait()
     dh[...], dl[...] = split(dinv[...])
     l_step(0)
     load_low.wait()
@@ -458,6 +461,9 @@
     first_half(near(2, 1))
     for b in range(1, 4):
         save_block(b)
+    first_rows = pl.ds(0, 8 * nb)
+    save_first = keep(blk.at[first_rows], a_out.at[first_rows])
+    pl.when(row != 0)(save_first.start)
     q_step(9, 2)
     for n, dx in enumerate((0, 3, 1, 2)):
         arrive("R", None, head(near(dx, 1), 0, 2), h_core + n)
@@ -503,7 +509,8 @@
         def _():
             put(0, 0, lambda here, t: cf[:, t * 128 : (t + 1) * 128])
 
-    save_block(0)
+    pl.when(row == 0)(save_first.start)
+    save_first.wait()
     q_finish()
     for cond, body in open_sends:
         when(cond, body)
@@ -527,9 +534,10 @@
             jax.ShapeDtypeStruct((2, nb, nb), BF),
             jax.ShapeDtypeStruct((2, nb, nb), BF),
         ),
-        in_specs=[anywhere, anywhere, anywhere, pl.BlockSpec(memory_space=pltpu.VMEM)],
+        in_specs=[anywhere] * 4,
         out_specs=(anywhere,) * 5,
         scratch_shapes=[
+            pltpu.VMEM((nb, nb), F32),
             pltpu.VMEM((4, part, 4, 128), F32),
             pltpu.VMEM((4, part, nb), F32),
             pltpu.VMEM((nb, nb), BF),

time: 102 us -> 101 us (level)
  the two profiles are of different devices: /device:TPU:28 before, /device:TPU:5 now
where the time goes in v8:
time: 101 us
  Pallas kernels  101 us (100%)
    pallas_call x1, Pallas kernels, gather(): pl.pallas_call(gather_kernel, out_shape=(jax.ShapeDtypeStruct(blocks.shap...  87.4 us
    pallas_call x1, Pallas kernels, update(): pl.pallas_call(update_kernel, grid=(4,), out_shape=jax.ShapeDtypeStruct(a...  13.2 us

profile of v8, /device:TPU:5, one launch (start us, length us, event | category | flops | bytes accessed | tf_op | source)
XLA Modules:
  0.0 100.5 jit_solution(4870681677270932979)
XLA Ops:
  0.0 87.4 %gather.1 = (f32[16384,128]{1,0:T(8,128)}, bf16[4,512,512]{2,1,0:T(8,128)(2,1)}, bf16[4,512,512]{2,1,0:T(8,128)(2,1)}, bf16[2,512,512]{2,1,0:T(8,128)(2,1)}, bf16[2,512,512]{2,1,0:T(8,128)(2,1)}) custom-call(f32[4,512,2,4,128]{4,3,2,1,0:T(4,128)} %bitcast.4, f32[16384,128]{1,0:T(8,128)} %bitcast.5, f32[4,512,512]{2,1,0:T(8,128)} %bitcast.6, f32[512,512]{1,0:T(8,128)} %dinv_in.1), custom_call_target="tpu_custom_call" | custom-call | tf_op jit(solution)/shard_map/gather/pallas_call | solution.py:528
  87.4 13.2 %update.1 = f32[16384,128]{1,0:T(8,128)} custom-call(f32[16384,128]{1,0:T(8,128)} %get-tuple-element.10.a, bf16[4,512,512]{2,1,0:T(8,128)(2,1)} %get-tuple-element.11.lh, bf16[4,512,512]{2,1,0:T(8,128)(2,1)} %get-tuple-element.12.ll, bf16[2,512,512]{2,1,0:T(8,128)(2,1)} %get-tuple-element.13.gh, bf16[2,512,512]{2,1,0:T(8,128)(2,1)} %get-tuple-element.14.gl), custom_call_target="tpu_custom_call" | custom-call | tf_op jit(solution)/shard_map/update/pallas_call | solution.py:589
